TPU v7x, 256 devices: a whole 4x4x8 slice. The times are simulated.
256 devices in a mesh: section: 16 (over z, x_hi), head: 4 (over y), key: 4 (over x_lo, core).
Axes of the slice: x: 4 (x_hi: 2, x_lo: 2; x = x_hi * 2 + x_lo), y: 4, z: 8, core: 2. Of those that a mesh axis runs over, the one named last changes fastest.
Arguments:
- queries: bfloat16 [16, 256, 3072], P('section', None, 'head'), may hold values from -1024 to 1024
- attn_grad: bfloat16 [16, 256, 3072], P('section', None, 'head'), may hold values from -192 to 192
- query_weight: bfloat16 [16, 3072, 3072], P('section', None, 'head'), may hold values from -0.109375 to 0.109375
- key_codes: int32 [4096, 1024], P('key', 'head'), may hold values from -127 to 127
- key_exps: int32 [64, 8], P('key', 'head'), may hold values from -9 to -6
- value_codes: int32 [4096, 1024], P('key', 'head'), may hold values from -127 to 127
- value_exps: int32 [64, 8], P('key', 'head'), may hold values from -9 to -6
Outputs:
- input_grad: bfloat16 [16, 256, 3072], P('section', ('head', 'key'))
- key_grad: float32 [4096, 1024], P(('key', 'section'), 'head')
- value_grad: float32 [4096, 1024], P(('key', 'section'), 'head')
All inputs are finite; a program needn't handle non-finite values.
Results may differ from a plain program's by a relative error of at most 0.017.
Values may be sent and summed in bfloat16 or wider, within the bound.
No kernel may reach another device: no remote copies, remote signals or barrier semaphores. Data moves between devices by JAX's collectives and lax.ppermute only.
A program may use at most 64 MiB of HBM per device.

v0:
```python
import jax
import jax.numpy as jnp
from jax import lax
from jax.experimental import pallas as pl
from jax.experimental.pallas import tpu as pltpu
from jax.sharding import PartitionSpec as P


HQ = 24
KVH = 8
HD = 128
GROUP = HQ // KVH
ROWS = 256
BLK = 64
LOG2E = 1.4426950408889634
SCALE = HD ** -0.5
LEAST_EXP = -9
DEPTH = 8
W_TILES = 6

F32 = jnp.float32
BF16 = jnp.bfloat16

VMEM = pl.BlockSpec(memory_space=pltpu.VMEM)
HBM = pl.BlockSpec(memory_space=pl.ANY)


def dot(a, b, dims):
    return lax.dot_general(a, b, (dims, ((), ())), preferred_element_type=F32)


def local_kernel(exps_k, exps_v, q_hbm, d_hbm, kc_hbm, vc_hbm,
                 e_ref, dp_ref, kt_ref, stat_ref, q_ref, d_ref,
                 kc_ref, vc_ref, k_ref, v_ref, ke_ref, ve_ref, sems):
    sources = (exps_k, exps_v, kc_hbm, q_hbm, vc_hbm, d_hbm)
    targets = (ke_ref, ve_ref, kc_ref, q_ref, vc_ref, d_ref)
    copies = [pltpu.make_async_copy(s, t, sems.at[n]) for n, (s, t) in enumerate(zip(sources, targets))]
    for c in copies:
        c.start()
    keys = kc_ref.shape[0]
    half = keys // 2

    def dequantize(exps, codes, out):
        for g in range(2):
            wide = slice(g * HD, (g + 1) * HD)
            for b in range(keys // BLK):
                at = slice(b * BLK, (b + 1) * BLK)
                power = jnp.left_shift(1, exps[g, b] - LEAST_EXP).astype(F32) * (2.0 ** LEAST_EXP)
                out[at, wide] = (codes[at, wide].astype(F32) * power).astype(BF16)

    copies[0].wait()
    copies[2].wait()
    dequantize(ke_ref, kc_ref, k_ref)
    copies[3].wait()
    for head in range(2 * GROUP):
        g = head // GROUP
        wide = slice(g * HD, (g + 1) * HD)
        cols = slice(head * HD, (head + 1) * HD)
        q = q_ref[:, cols]
        if head == 0:
            copies[1].wait()
            copies[4].wait()
            dequantize(ve_ref, vc_ref, v_ref)
            copies[5].wait()
        d = d_ref[:, cols]
        top = None
        for c in range(2):
            at = slice(c * half, (c + 1) * half)
            s = dot(k_ref[at, wide], q, ((1,), (1,)))
            dp_ref[head, at, :] = s
            part = jnp.max(s, axis=0, keepdims=True)
            top = part if top is None else jnp.maximum(top, part)
        total = jnp.zeros((1, ROWS), F32)
        inner = jnp.zeros((1, ROWS), F32)
        for c in range(2):
            at = slice(c * half, (c + 1) * half)
            e = jnp.exp2((dp_ref[head, at, :] - top) * (SCALE * LOG2E))
            e_ref[head, at, :] = e
            total += jnp.sum(e, axis=0, keepdims=True)
            dp = dot(v_ref[at, wide], d, ((1,), (1,)))
            dp_ref[head, at, :] = dp
            inner += jnp.sum(e * dp, axis=0, keepdims=True)
        stat_ref[head:head + 1, :] = top * (SCALE * LOG2E)
        stat_ref[8 + head:9 + head, :] = total
        stat_ref[16 + head:17 + head, :] = inner
    for g in range(2):
        wide = slice(g * HD, (g + 1) * HD)
        kt_ref[wide, :] = k_ref[:, wide].T


def cache_grad_kernel(*refs):
    stats, (e_ref, dp_ref, q_ref, d_ref, ds_ref, keep_ref, send_v, send_k, both) = refs[:4], refs[4:]
    top = stats[0][0:8, :]
    for s in stats[1:]:
        top = jnp.maximum(top, s[0:8, :])
    weights = [jnp.exp2(s[0:8, :] - top) for s in stats]
    total = sum(w * s[8:16, :] for w, s in zip(weights, stats))
    inner = sum(w * s[16:24, :] for w, s in zip(weights, stats))
    delta = inner / total
    mine = weights[0] / total
    slab = both.shape[2]
    for g in range(2):
        for h in range(GROUP):
            head = g * GROUP + h
            cols = slice(head * HD, (head + 1) * HD)
            p = e_ref[head] * mine[head:head + 1, :]
            ds = (p * (dp_ref[head] - delta[head:head + 1, :])).astype(BF16)
            ds_ref[head] = ds
            kg = dot(ds, q_ref[:, cols], ((1,), (0,)))
            vg = dot(p.astype(BF16), d_ref[:, cols], ((1,), (0,)))
            key_sum = kg if h == 0 else key_sum + kg
            value_sum = vg if h == 0 else value_sum + vg
        key_low = (key_sum * SCALE).astype(BF16)
        value_low = value_sum.astype(BF16)
        for z in range(DEPTH):
            at = slice(z * slab, (z + 1) * slab)
            both[z % 2, z // 2, :, g * HD:(g + 1) * HD] = key_low[at, :]
            both[z % 2, z // 2, :, (2 + g) * HD:(3 + g) * HD] = value_low[at, :]
    side = lax.rem(lax.axis_index("section") // 2, 2)
    keep_ref[...] = both[side]
    send_k[...] = both[1 - side, :, :, :2 * HD]
    send_v[...] = both[1 - side, :, :, 2 * HD:]


def query_grad_kernel(ds_ref, kt_ref, o0, o1, o2, o3, all_ref):
    for head in range(2 * GROUP):
        g = head // GROUP
        cols = slice(head * HD, (head + 1) * HD)
        qt = dot(kt_ref[g * HD:(g + 1) * HD, :], ds_ref[head], ((1,), (0,)))
        qg = (qt.T * SCALE).astype(BF16)
        for a in range(4):
            for k in range(4):
                all_ref[k, a * 16:(a + 1) * 16, cols] = qg[(a * 4 + k) * 16:(a * 4 + k + 1) * 16, :]
    me = lax.axis_index("key")
    for by, o in enumerate((o0, o1, o2, o3)):
        o[...] = all_ref[jnp.bitwise_xor(me, by)]


def pair_kernel(keep_ref, key_ref, value_ref, out_ref):
    w = key_ref.shape[-1]
    out_ref[:, :, :w] = (keep_ref[:, :, :w].astype(F32) + key_ref[...].astype(F32)).astype(BF16)
    out_ref[:, :, w:] = (keep_ref[:, :, w:].astype(F32) + value_ref[...].astype(F32)).astype(BF16)


def project_kernel(a_ref, b_ref, c_ref, d_ref, w_ref, o0, o1, o2, o3, all_ref):
    total = sum(r[...].astype(F32) for r in (a_ref, b_ref, c_ref, d_ref)).astype(BF16)
    tile = w_ref.shape[0] // W_TILES
    for n in range(W_TILES):
        at = slice(n * tile, (n + 1) * tile)
        part = dot(total, w_ref[at, :], ((1,), (1,))).astype(BF16)
        for k in range(4):
            all_ref[k, :, at] = part[k * 16:(k + 1) * 16, :]
    me = lax.axis_index("head")
    for by, o in enumerate((o0, o1, o2, o3)):
        o[...] = all_ref[lax.rem(me + by, 4)]


def finish_kernel(kv_ref, a_ref, b_ref, c_ref, d_ref, key_ref, value_ref, input_ref):
    total = kv_ref[0].astype(F32)
    for k in range(1, kv_ref.shape[0]):
        total += kv_ref[k].astype(F32)
    width = key_ref.shape[1]
    key_ref[...] = total[:, :width]
    value_ref[...] = total[:, width:]
    input_ref[...] = sum(r[...].astype(F32) for r in (a_ref, b_ref, c_ref, d_ref)).astype(BF16)


def moved(x, axis, to):
    return lax.ppermute(x, axis, [(i, to(i)) for i in range(lax.axis_size(axis))])


def deeper(section, by):
    return (section // 2 + by) % DEPTH * 2 + section % 2


def call(kernel, outs, ins, scratch=(), limit=16, specs=None, cost=1 << 28):
    return pl.pallas_call(
        kernel,
        in_specs=specs or [VMEM] * len(ins),
        out_specs=[VMEM] * len(outs),
        out_shape=outs,
        scratch_shapes=scratch,
        compiler_params=pltpu.CompilerParams(vmem_limit_bytes=limit << 20),
        cost_estimate=pl.CostEstimate(flops=cost, bytes_accessed=1 << 20, transcendentals=0),
    )(*ins)


def step(queries, attn_grad, query_weight, key_codes, key_exps, value_codes, value_exps):
    q, d, w = queries[0], attn_grad[0], query_weight[0]
    keys, width = key_codes.shape
    heads = q.shape[1] // HD
    d_model = w.shape[0]
    on = pltpu.VMEM
    e, dp, kt, stat, q, d = call(
        local_kernel,
        [on((heads, keys, ROWS), F32), on((heads, keys, ROWS), F32), on((width, keys), BF16),
         on((24, ROWS), F32), on(q.shape, BF16), on(d.shape, BF16)],
        [pltpu.with_memory_space_constraint(x, pltpu.HBM)
         for x in (key_exps.T, value_exps.T, q, d, key_codes, value_codes)],
        scratch=[on(key_codes.shape, jnp.int32), on(key_codes.shape, jnp.int32),
                 on(key_codes.shape, BF16), on(key_codes.shape, BF16),
                 pltpu.SMEM(key_exps.shape[::-1], jnp.int32), pltpu.SMEM(key_exps.shape[::-1], jnp.int32),
                 pltpu.SemaphoreType.DMA((6,))],
        limit=16, specs=[HBM] * 6,
    )
    stats = [stat] + [moved(stat, "key", lambda i: i ^ by) for by in (1, 2, 3)]
    slab = keys // DEPTH
    half = (DEPTH // 2, slab, width)
    ds, keep, send_v, send_k = call(
        cache_grad_kernel,
        [on((heads, keys, ROWS), BF16), on((*half[:2], 2 * width), BF16), on(half, BF16), on(half, BF16)],
        (*stats, e, dp, q, d),
        scratch=[on((2, *half[:2], 2 * width), BF16)],
    )
    got_v = moved(send_v, "section", lambda i: deeper(i, 1 - 2 * (i // 2 % 2)))
    got_k = moved(send_k, "section", lambda i: deeper(i, 2 * (i // 2 % 2) - 1))
    rows = ROWS // 4
    parts = call(
        query_grad_kernel,
        [on((rows, heads * HD), BF16)] * 4, (ds, kt),
        scratch=[on((4, rows, heads * HD), BF16)],
    )
    keep, parts = lax.optimization_barrier((keep, parts))
    parts = [parts[0]] + [moved(parts[by], "key", lambda i: i ^ by) for by in (1, 2, 3)]
    (kv,) = call(pair_kernel, [jax.ShapeDtypeStruct((*half[:2], 2 * width), BF16)], (keep, got_k, got_v))
    groups = [[(2 * a + p) * 2 + xh for a in range(DEPTH // 2) for xh in range(2)] for p in range(2)]
    kv = lax.all_to_all(kv.reshape(DEPTH, slab // 2, 2 * width), "section", 0, 0, axis_index_groups=groups, tiled=True)
    parts = call(
        project_kernel, [on((rows // 4, d_model), BF16)] * 4, (*parts, w), scratch=[on((4, rows // 4, d_model), BF16)]
    )
    parts = [parts[0]] + [moved(parts[by], "head", lambda i: (i + by) % 4) for by in (1, 2, 3)]
    key_grad, value_grad, input_grad = call(
        finish_kernel,
        [jax.ShapeDtypeStruct((slab // 2, width), F32), jax.ShapeDtypeStruct((slab // 2, width), F32),
         jax.ShapeDtypeStruct((rows // 4, d_model), BF16)],
        (kv, *parts),
    )
    return input_grad[None], key_grad, value_grad


def solution(mesh):
    return jax.shard_map(
        step,
        mesh=mesh,
        in_specs=(
            P("section", None, "head"),
            P("section", None, "head"),
            P("section", None, "head"),
            P("key", "head"),
            P("key", "head"),
            P("key", "head"),
            P("key", "head"),
        ),
        out_specs=(
            P("section", ("head", "key"), None),
            P(("key", "section"), "head"),
            P(("key", "section"), "head"),
        ),
        check_vma=False,
    )
```

profile of v0, /device:TPU:8, one launch (start us, length us, event | category | flops | bytes accessed | tf_op | source)
XLA Modules:
  0.0 56.7 jit_solution(13339294838679099848)
XLA Ops:
  0.6 4.1 %shard_map.94 = (f32[6,1024,256]{2,1,0:T(8,128)S(1)}, f32[6,1024,256]{2,1,0:T(8,128)S(1)}, bf16[256,1024]{1,0:T(8,128)(2,1)S(1)}, f32[24,256]{1,0:T(8,128)S(1)},...) custom-call(s32[2,16]{1,0:T(2,128)} %bitcast.10, s32[2,16]{1,0:T(2,128)} %bitcast.11, ...), custom_call_target="tpu_custom_call" | custom-call | flops 268435456 | bytes 1048576 | tf_op jit(solution)/shard_map/pallas_call | solution.py:177
  4.8 1.0 %collective-permute-start.2 = (f32[24,256]{1,0:T(8,128)S(1)}, f32[24,256]{1,0:T(8,128)S(1)}, u32[]{:S(2)}, u32[]{:S(2)}) collective-permute-start(f32[24,256]{1,0:T(8,128)S(1)} %get-tuple-element.29.refs_0_), channel_id=1, source_target_pairs={{0,3},{1,2},{2,1},{3,0},{4,7},{5,6},{6,5},{7,4},{8,11},{9,10},{10,... | collective-permute-start | bytes 73736 | tf_op jit(solution)/shard_map/ppermute | solution.py:169
  5.8 0.7 %collective-permute-start.1 = (f32[24,256]{1,0:T(8,128)S(1)}, f32[24,256]{1,0:T(8,128)S(1)}, u32[]{:S(2)}, u32[]{:S(2)}) collective-permute-start(f32[24,256]{1,0:T(8,128)S(1)} %get-tuple-element.29.refs_0_), channel_id=1, source_target_pairs={{0,2},{1,3},{2,0},{3,1},{4,6},{5,7},{6,4},{7,5},{8,10},{9,11},{10,... | collective-permute-start | bytes 73736 | tf_op jit(solution)/shard_map/ppermute | solution.py:169
  6.7 1.6 %collective-permute-done.2.refs_3_ = f32[24,256]{1,0:T(8,128)S(1)} collective-permute-done((f32[24,256]{1,0:T(8,128)S(1)}, f32[24,256]{1,0:T(8,128)S(1)}, u32[]{:S(2)}, u32[]{:S(2)}) %collective-permute-start.2) | collective-permute-done | bytes 24608 | tf_op jit(solution)/shard_map/ppermute | solution.py:169
  8.3 1.3 %collective-permute-done.1.refs_2_ = f32[24,256]{1,0:T(8,128)S(1)} collective-permute-done((f32[24,256]{1,0:T(8,128)S(1)}, f32[24,256]{1,0:T(8,128)S(1)}, u32[]{:S(2)}, u32[]{:S(2)}) %collective-permute-start.1) | collective-permute-done | bytes 24608 | tf_op jit(solution)/shard_map/ppermute | solution.py:169
  9.6 2.1 %shard_map.95 = (bf16[6,1024,256]{2,1,0:T(8,128)(2,1)S(1)}, bf16[4,128,512]{2,1,0:T(8,128)(2,1)S(1)}, bf16[4,128,256]{2,1,0:T(8,128)(2,1)S(1)}, bf16[4,128,256]{2,1,0:T(8,128)(2,1)S(1)}) custom-call(f32[24,256]{1,0:T(8,128)S(1)} %get-tuple-element.29.refs_0_, f32[24,256]{1,0:T(8,128)S(1)} %collective-permute-done.refs_1_, ...), custom_call_target="tpu_custom_call" | custom-call | flops 268435456 | bytes 1048576 | tf_op jit(solution)/shard_map/pallas_call | solution.py:177
  11.7 5.9 %collective-permute-start.3 = (bf16[4,128,256]{2,1,0:T(8,128)(2,1)S(1)}, bf16[4,128,256]{2,1,0:T(8,128)(2,1)S(1)}, u32[]{:S(2)}, u32[]{:S(2)}) collective-permute-start(bf16[4,128,256]{2,1,0:T(8,128)(2,1)S(1)} %get-tuple-element.42), channel_id=1, source_target_pairs={{0,224},{16,240},{32,64},{48,80},{64,32},{80,48},{96,128},{112,144... | collective-permute-start | bytes 786440 | tf_op jit(solution)/shard_map/ppermute | solution.py:169
  17.7 0.7 %shard_map.96 = (bf16[64,768]{1,0:T(8,128)(2,1)S(1)}, bf16[64,768]{1,0:T(8,128)(2,1)S(1)}, bf16[64,768]{1,0:T(8,128)(2,1)S(1)}, bf16[64,768]{1,0:T(8,128)(2,1)S(1)}) custom-call(bf16[6,1024,256]{2,1,0:T(8,128)(2,1)S(1)} %get-tuple-element.35.ds_ref, bf16[256,1024]{1,0:T(8,128)(2,1)S(1)} %get-tuple-element.36.kt_ref), custom_call_target="tpu_custom_call" | custom-call | flops 268435456 | bytes 1048576 | tf_op jit(solution)/shard_map/pallas_call | solution.py:177
  18.4 5.3 %collective-permute-done.3.key_ref = bf16[4,128,256]{2,1,0:T(8,128)(2,1)S(1)} collective-permute-done((bf16[4,128,256]{2,1,0:T(8,128)(2,1)S(1)}, bf16[4,128,256]{2,1,0:T(8,128)(2,1)S(1)}, u32[]{:S(2)}, u32[]{:S(2)}) %collective-permute-start.3) | collective-permute-done | bytes 262176 | tf_op jit(solution)/shard_map/ppermute | solution.py:169
  23.7 1.5 %collective-permute-done.4.value_ref = bf16[4,128,256]{2,1,0:T(8,128)(2,1)S(1)} collective-permute-done((bf16[4,128,256]{2,1,0:T(8,128)(2,1)S(1)}, bf16[4,128,256]{2,1,0:T(8,128)(2,1)S(1)}, u32[]{:S(2)}, u32[]{:S(2)}) %collective-permute-start.4) | collective-permute-done | bytes 262176 | tf_op jit(solution)/shard_map/ppermute | solution.py:169
  25.1 0.9 %shard_map.97 = bf16[4,128,512]{2,1,0:T(8,128)(2,1)} custom-call(bf16[4,128,512]{2,1,0:T(8,128)(2,1)S(1)} %get-tuple-element.41.keep_ref, bf16[4,128,256]{2,1,0:T(8,128)(2,1)S(1)} %collective-permute-done.3.key_ref, bf16[4,128,256]{2,1,0:T(8,128)(2,1)S(1)} %collective-permute-done.4.value_ref), custom_call_target="tpu_custom_call" | custom-call | flops 268435456 | bytes 1048576 | tf_op jit(solution)/shard_map/pallas_call | solution.py:177
  26.0 6.3 %all-to-all-start = ((bf16[8,64,512]{2,1,0:T(8,128)(2,1)}), bf16[8,64,512]{2,1,0:T(8,128)(2,1)S(1)}, u32[]{:S(2)}, u32[]{:S(2)}) async-start(bf16[8,64,512]{2,1,0:T(8,128)(2,1)} %bitcast.4), calls=%async_computation | async-start | bytes 1048576 | tf_op jit(solution)/shard_map/all_to_all | solution.py:227
  32.3 0.3 collective-permute-start.6
  32.6 1.5 %collective-permute-start.7 = (bf16[64,768]{1,0:T(8,128)(2,1)S(1)}, bf16[64,768]{1,0:T(8,128)(2,1)S(1)}, u32[]{:S(2)}, u32[]{:S(2)}) collective-permute-start(bf16[64,768]{1,0:T(8,128)(2,1)S(1)} %get-tuple-element.47), channel_id=1, source_target_pairs={{0,3},{1,2},{2,1},{3,0},{4,7},{5,6},{6,5},{7,4},{8,11},{9,10},{10,... | collective-permute-start | bytes 294920 | tf_op jit(solution)/shard_map/ppermute | solution.py:169
  34.2 4.3 %collective-permute-done.6.c_ref = bf16[64,768]{1,0:T(8,128)(2,1)S(1)} collective-permute-done((bf16[64,768]{1,0:T(8,128)(2,1)S(1)}, bf16[64,768]{1,0:T(8,128)(2,1)S(1)}, u32[]{:S(2)}, u32[]{:S(2)}) %collective-permute-start.6) | collective-permute-done | bytes 98336 | tf_op jit(solution)/shard_map/ppermute | solution.py:169
  38.5 4.4 %collective-permute-done.7.d_ref = bf16[64,768]{1,0:T(8,128)(2,1)S(1)} collective-permute-done((bf16[64,768]{1,0:T(8,128)(2,1)S(1)}, bf16[64,768]{1,0:T(8,128)(2,1)S(1)}, u32[]{:S(2)}, u32[]{:S(2)}) %collective-permute-start.7) | collective-permute-done | bytes 98336 | tf_op jit(solution)/shard_map/ppermute | solution.py:169
  42.9 2.3 %copy-done = bf16[1,3072,768]{2,1,0:T(8,128)(2,1)S(1)} copy-done((bf16[1,3072,768]{2,1,0:T(8,128)(2,1)S(1)}, bf16[1,3072,768]{2,1,0:T(8,128)(2,1)}, u32[]{:S(2)}) %copy-start) | copy-done | bytes 4718616
  45.3 1.5 %shard_map.98 = (bf16[16,3072]{1,0:T(8,128)(2,1)S(1)}, bf16[16,3072]{1,0:T(8,128)(2,1)S(1)}, bf16[16,3072]{1,0:T(8,128)(2,1)S(1)}, bf16[16,3072]{1,0:T(8,128)(2,1)S(1)}) custom-call(bf16[64,768]{1,0:T(8,128)(2,1)S(1)} %get-tuple-element.44.a_ref, bf16[64,768]{1,0:T(8,128)(2,1)S(1)} %collective-permute-done.5.b_ref, ...), custom_call_target="tpu_custom_call" | custom-call | flops 268435456 | bytes 1048576 | tf_op jit(solution)/shard_map/pallas_call | solution.py:177
  46.8 1.7 %collective-permute-start.8 = (bf16[16,3072]{1,0:T(8,128)(2,1)S(1)}, bf16[16,3072]{1,0:T(8,128)(2,1)S(1)}, u32[]{:S(2)}, u32[]{:S(2)}) collective-permute-start(bf16[16,3072]{1,0:T(8,128)(2,1)S(1)} %get-tuple-element.49), channel_id=1, source_target_pairs={{0,4},{4,8},{8,12},{12,0},{1,5},{5,9},{9,13},{13,1},{2,6},{6,10},{... | collective-permute-start | bytes 294920 | tf_op jit(solution)/shard_map/ppermute | solution.py:169
  48.5 1.0 %collective-permute-start.9 = (bf16[16,3072]{1,0:T(8,128)(2,1)S(1)}, bf16[16,3072]{1,0:T(8,128)(2,1)S(1)}, u32[]{:S(2)}, u32[]{:S(2)}) collective-permute-start(bf16[16,3072]{1,0:T(8,128)(2,1)S(1)} %get-tuple-element.50), channel_id=1, source_target_pairs={{0,8},{4,12},{8,0},{12,4},{1,9},{5,13},{9,1},{13,5},{2,10},{6,14},... | collective-permute-start | bytes 294920 | tf_op jit(solution)/shard_map/ppermute | solution.py:169
  49.4 2.4 %collective-permute-start.10 = (bf16[16,3072]{1,0:T(8,128)(2,1)S(1)}, bf16[16,3072]{1,0:T(8,128)(2,1)S(1)}, u32[]{:S(2)}, u32[]{:S(2)}) collective-permute-start(bf16[16,3072]{1,0:T(8,128)(2,1)S(1)} %get-tuple-element.51), channel_id=1, source_target_pairs={{0,12},{4,0},{8,4},{12,8},{1,13},{5,1},{9,5},{13,9},{2,14},{6,2},{... | collective-permute-start | bytes 294920 | tf_op jit(solution)/shard_map/ppermute | solution.py:169
  51.8 3.8 %collective-permute-done.9.c_ref = bf16[16,3072]{1,0:T(8,128)(2,1)S(1)} collective-permute-done((bf16[16,3072]{1,0:T(8,128)(2,1)S(1)}, bf16[16,3072]{1,0:T(8,128)(2,1)S(1)}, u32[]{:S(2)}, u32[]{:S(2)}) %collective-permute-start.9) | collective-permute-done | bytes 98336 | tf_op jit(solution)/shard_map/ppermute | solution.py:169
  55.6 0.3 collective-permute-done.10.d_ref
  56.0 0.8 %shard_map.99 = (f32[64,256]{1,0:T(8,128)}, f32[64,256]{1,0:T(8,128)}, bf16[16,3072]{1,0:T(8,128)(2,1)}) custom-call(bf16[8,64,512]{2,1,0:T(8,128)(2,1)S(1)} %all-to-all-done.kv_ref, bf16[16,3072]{1,0:T(8,128)(2,1)S(1)} %get-tuple-element.48.a_ref, bf16[16,3072]{1,0:T(8,128)(2,1)S(1)} %collective-permute-done.8.b_ref, ...), custom_call_target="tpu_custom_call" | custom-call | flops 268435456 | bytes 1048576 | tf_op jit(solution)/shard_map/pallas_call | solution.py:177
  (8 shorter events, 0.3 us)
Async XLA Ops:
  4.8 3.6 %collective-permute-start.2 = (f32[24,256]{1,0:T(8,128)S(1)}, f32[24,256]{1,0:T(8,128)S(1)}, u32[]{:S(2)}, u32[]{:S(2)}) collective-permute-start(f32[24,256]{1,0:T(8,128)S(1)} %get-tuple-element.29.refs_0_), channel_id=1, source_target_pairs={{0,3},{1,2},{2,1},{3,0},{4,7},{5,6},{6,5},{7,4},{8,11},{9,10},{10,... | collective-permute-start | bytes 73736 | tf_op jit(solution)/shard_map/ppermute | solution.py:169
  5.8 3.8 %collective-permute-start.1 = (f32[24,256]{1,0:T(8,128)S(1)}, f32[24,256]{1,0:T(8,128)S(1)}, u32[]{:S(2)}, u32[]{:S(2)}) collective-permute-start(f32[24,256]{1,0:T(8,128)S(1)} %get-tuple-element.29.refs_0_), channel_id=1, source_target_pairs={{0,2},{1,3},{2,0},{3,1},{4,6},{5,7},{6,4},{7,5},{8,10},{9,11},{10,... | collective-permute-start | bytes 73736 | tf_op jit(solution)/shard_map/ppermute | solution.py:169
  6.5 3.2 %collective-permute-start = (f32[24,256]{1,0:T(8,128)S(1)}, f32[24,256]{1,0:T(8,128)S(1)}, u32[]{:S(2)}, u32[]{:S(2)}) collective-permute-start(f32[24,256]{1,0:T(8,128)S(1)} %get-tuple-element.29.refs_0_), channel_id=1, source_target_pairs={{0,1},{1,0},{2,3},{3,2},{4,5},{5,4},{6,7},{7,6},{8,9},{9,8},{10,11... | collective-permute-start | bytes 73736 | tf_op jit(solution)/shard_map/ppermute | solution.py:169
  11.7 11.9 %collective-permute-start.3 = (bf16[4,128,256]{2,1,0:T(8,128)(2,1)S(1)}, bf16[4,128,256]{2,1,0:T(8,128)(2,1)S(1)}, u32[]{:S(2)}, u32[]{:S(2)}) collective-permute-start(bf16[4,128,256]{2,1,0:T(8,128)(2,1)S(1)} %get-tuple-element.42), channel_id=1, source_target_pairs={{0,224},{16,240},{32,64},{48,80},{64,32},{80,48},{96,128},{112,144... | collective-permute-start | bytes 786440 | tf_op jit(solution)/shard_map/ppermute | solution.py:169
  17.7 7.5 %collective-permute-start.4 = (bf16[4,128,256]{2,1,0:T(8,128)(2,1)S(1)}, bf16[4,128,256]{2,1,0:T(8,128)(2,1)S(1)}, u32[]{:S(2)}, u32[]{:S(2)}) collective-permute-start(bf16[4,128,256]{2,1,0:T(8,128)(2,1)S(1)} %get-tuple-element.43), channel_id=1, source_target_pairs={{0,32},{16,48},{32,0},{48,16},{64,96},{80,112},{96,64},{112,80},{1... | collective-permute-start | bytes 786440 | tf_op jit(solution)/shard_map/ppermute | solution.py:169
  26.0 29.9 %all-to-all-start = ((bf16[8,64,512]{2,1,0:T(8,128)(2,1)}), bf16[8,64,512]{2,1,0:T(8,128)(2,1)S(1)}, u32[]{:S(2)}, u32[]{:S(2)}) async-start(bf16[8,64,512]{2,1,0:T(8,128)(2,1)} %bitcast.4), calls=%async_computation | async-start | bytes 1048576 | tf_op jit(solution)/shard_map/all_to_all | solution.py:227
  32.3 1.9 %collective-permute-start.5 = (bf16[64,768]{1,0:T(8,128)(2,1)S(1)}, bf16[64,768]{1,0:T(8,128)(2,1)S(1)}, u32[]{:S(2)}, u32[]{:S(2)}) collective-permute-start(bf16[64,768]{1,0:T(8,128)(2,1)S(1)} %get-tuple-element.45), channel_id=1, source_target_pairs={{0,1},{1,0},{2,3},{3,2},{4,5},{5,4},{6,7},{7,6},{8,9},{9,8},{10,11... | collective-permute-start | bytes 294920 | tf_op jit(solution)/shard_map/ppermute | solution.py:169
  32.3 6.2 %collective-permute-start.6 = (bf16[64,768]{1,0:T(8,128)(2,1)S(1)}, bf16[64,768]{1,0:T(8,128)(2,1)S(1)}, u32[]{:S(2)}, u32[]{:S(2)}) collective-permute-start(bf16[64,768]{1,0:T(8,128)(2,1)S(1)} %get-tuple-element.46), channel_id=1, source_target_pairs={{0,2},{1,3},{2,0},{3,1},{4,6},{5,7},{6,4},{7,5},{8,10},{9,11},{10,... | collective-permute-start | bytes 294920 | tf_op jit(solution)/shard_map/ppermute | solution.py:169
  32.6 10.3 %collective-permute-start.7 = (bf16[64,768]{1,0:T(8,128)(2,1)S(1)}, bf16[64,768]{1,0:T(8,128)(2,1)S(1)}, u32[]{:S(2)}, u32[]{:S(2)}) collective-permute-start(bf16[64,768]{1,0:T(8,128)(2,1)S(1)} %get-tuple-element.47), channel_id=1, source_target_pairs={{0,3},{1,2},{2,1},{3,0},{4,7},{5,6},{6,5},{7,4},{8,11},{9,10},{10,... | collective-permute-start | bytes 294920 | tf_op jit(solution)/shard_map/ppermute | solution.py:169
  42.9 2.3 %copy-start = (bf16[1,3072,768]{2,1,0:T(8,128)(2,1)S(1)}, bf16[1,3072,768]{2,1,0:T(8,128)(2,1)}, u32[]{:S(2)}) copy-start(bf16[1,3072,768]{2,1,0:T(8,128)(2,1)} %param.9) | copy-start | bytes 14155780
  46.8 5.0 %collective-permute-start.8 = (bf16[16,3072]{1,0:T(8,128)(2,1)S(1)}, bf16[16,3072]{1,0:T(8,128)(2,1)S(1)}, u32[]{:S(2)}, u32[]{:S(2)}) collective-permute-start(bf16[16,3072]{1,0:T(8,128)(2,1)S(1)} %get-tuple-element.49), channel_id=1, source_target_pairs={{0,4},{4,8},{8,12},{12,0},{1,5},{5,9},{9,13},{13,1},{2,6},{6,10},{... | collective-permute-start | bytes 294920 | tf_op jit(solution)/shard_map/ppermute | solution.py:169
  48.5 7.2 %collective-permute-start.9 = (bf16[16,3072]{1,0:T(8,128)(2,1)S(1)}, bf16[16,3072]{1,0:T(8,128)(2,1)S(1)}, u32[]{:S(2)}, u32[]{:S(2)}) collective-permute-start(bf16[16,3072]{1,0:T(8,128)(2,1)S(1)} %get-tuple-element.50), channel_id=1, source_target_pairs={{0,8},{4,12},{8,0},{12,4},{1,9},{5,13},{9,1},{13,5},{2,10},{6,14},... | collective-permute-start | bytes 294920 | tf_op jit(solution)/shard_map/ppermute | solution.py:169
  49.4 6.6 %collective-permute-start.10 = (bf16[16,3072]{1,0:T(8,128)(2,1)S(1)}, bf16[16,3072]{1,0:T(8,128)(2,1)S(1)}, u32[]{:S(2)}, u32[]{:S(2)}) collective-permute-start(bf16[16,3072]{1,0:T(8,128)(2,1)S(1)} %get-tuple-element.51), channel_id=1, source_target_pairs={{0,12},{4,0},{8,4},{12,8},{1,13},{5,1},{9,5},{13,9},{2,14},{6,2},{... | collective-permute-start | bytes 294920 | tf_op jit(solution)/shard_map/ppermute | solution.py:169
where the time goes:
time: 57.6 us; the launch traced here: 56.7 us
  waiting for transfers between devices  22.6 us (39%)
  starting transfers between devices  21 us (36%)
  Pallas kernels  10.1 us (18%)
  local copies, waits for them, and re-layouts  2.34 us (4%)
  between operations  0.67 us (1%)
    ppermute x11, waiting for transfers between devices, moved(): lax.ppermute(x, axis, [(i, to(i)) for i in range(lax.axis_size(axis))])  22.6 us
    ppermute x11, starting transfers between devices, moved(): lax.ppermute(x, axis, [(i, to(i)) for i in range(lax.axis_size(axis))])  14.8 us
    pallas_call x6, Pallas kernels, call(): pl.pallas_call(kernel, in_specs=specs or [VMEM] * len(ins), out_specs=[VM...  10.1 us
    all_to_all x1, starting transfers between devices, step(): lax.all_to_all(kv.reshape(DEPTH, slab // 2, 2 * width), 'section', 0, 0,...  6.27 us
    unnamed x2, local copies, waits for them, and re-layouts  2.34 us
  transfers between devices with their start and end apart: 12, of which 8 were waited for; matrix products, arithmetic and copies ran while one was open for 0% of the time, Pallas kernels for 4%

commit v1 on v0

--- a/solution.py
+++ b/solution.py
@@ -1,3 +1,5 @@
+import functools
+
 import jax
 import jax.numpy as jnp
 from jax import lax
@@ -29,13 +31,13 @@
     return lax.dot_general(a, b, (dims, ((), ())), preferred_element_type=F32)
 
 
-def local_kernel(exps_k, exps_v, q_hbm, d_hbm, kc_hbm, vc_hbm,
-                 e_ref, dp_ref, kt_ref, stat_ref, q_ref, d_ref,
+def local_kernel(exps_k, exps_v, q_hbm, d_hbm, kc_hbm, vc_hbm, w_hbm,
+                 e_ref, dp_ref, kt_ref, stat_ref, q_ref, d_ref, w_ref,
                  kc_ref, vc_ref, k_ref, v_ref, ke_ref, ve_ref, sems):
-    sources = (exps_k, exps_v, kc_hbm, q_hbm, vc_hbm, d_hbm)
-    targets = (ke_ref, ve_ref, kc_ref, q_ref, vc_ref, d_ref)
+    sources = (exps_k, exps_v, kc_hbm, q_hbm, vc_hbm, d_hbm, w_hbm)
+    targets = (ke_ref, ve_ref, kc_ref, q_ref, vc_ref, d_ref, w_ref)
     copies = [pltpu.make_async_copy(s, t, sems.at[n]) for n, (s, t) in enumerate(zip(sources, targets))]
-    for c in copies:
+    for c in copies[:6]:
         c.start()
     keys = kc_ref.shape[0]
     half = keys // 2
@@ -62,6 +64,7 @@
             copies[4].wait()
             dequantize(ve_ref, vc_ref, v_ref)
             copies[5].wait()
+            copies[6].start()
         d = d_ref[:, cols]
         top = None
         for c in range(2):
@@ -86,10 +89,11 @@
     for g in range(2):
         wide = slice(g * HD, (g + 1) * HD)
         kt_ref[wide, :] = k_ref[:, wide].T
+    copies[6].wait()
 
 
 def cache_grad_kernel(*refs):
-    stats, (e_ref, dp_ref, q_ref, d_ref, ds_ref, keep_ref, send_v, send_k, both) = refs[:4], refs[4:]
+    stats, (e_ref, dp_ref, q_ref, d_ref, ds_ref, kv_ref, far_k, far_v) = refs[:4], refs[4:]
     top = stats[0][0:8, :]
     for s in stats[1:]:
         top = jnp.maximum(top, s[0:8, :])
@@ -98,7 +102,7 @@
     inner = sum(w * s[16:24, :] for w, s in zip(weights, stats))
     delta = inner / total
     mine = weights[0] / total
-    slab = both.shape[2]
+    slab = kv_ref.shape[1]
     for g in range(2):
         for h in range(GROUP):
             head = g * GROUP + h
@@ -114,12 +118,43 @@
         value_low = value_sum.astype(BF16)
         for z in range(DEPTH):
             at = slice(z * slab, (z + 1) * slab)
-            both[z % 2, z // 2, :, g * HD:(g + 1) * HD] = key_low[at, :]
-            both[z % 2, z // 2, :, (2 + g) * HD:(3 + g) * HD] = value_low[at, :]
-    side = lax.rem(lax.axis_index("section") // 2, 2)
-    keep_ref[...] = both[side]
-    send_k[...] = both[1 - side, :, :, :2 * HD]
-    send_v[...] = both[1 - side, :, :, 2 * HD:]
+            kv_ref[z, :, g * HD:(g + 1) * HD] = key_low[at, :]
+            kv_ref[z, :, (2 + g) * HD:(3 + g) * HD] = value_low[at, :]
+    far = away(DEPTH // 2)
+    far_k[...] = kv_ref[far, :, :2 * HD]
+    far_v[...] = kv_ref[far, :, 2 * HD:]
+
+
+def away(by):
+    return lax.rem(lax.axis_index("section") // 2 + (by + DEPTH), DEPTH)
+
+
+def added(*terms):
+    return sum(t.astype(F32) for t in terms).astype(BF16)
+
+
+def join_far_kernel(kv_ref, up_ref, down_ref, to_up, to_down):
+    w = up_ref.shape[1]
+    above, below = away(3), away(-3)
+    to_up[:, :w] = kv_ref[above, :, :w]
+    to_up[:, w:] = added(kv_ref[above, :, w:], up_ref[...])
+    to_down[:, :w] = added(kv_ref[below, :, :w], down_ref[...])
+    to_down[:, w:] = kv_ref[below, :, w:]
+
+
+def join_kernel(by, kv_ref, up_ref, down_ref, to_up, to_down):
+    to_up[...] = added(kv_ref[away(by)], up_ref[...])
+    to_down[...] = added(kv_ref[away(-by)], down_ref[...])
+
+
+def last_join_kernel(kv_ref, up_ref, down_ref, keep_ref, send_ref, both):
+    rows = keep_ref.shape[0]
+    mine = kv_ref[away(0)].astype(F32) + up_ref[...].astype(F32) + down_ref[...].astype(F32)
+    both[0] = mine[:rows]
+    both[1] = mine[rows:]
+    part = lax.rem(lax.axis_index("section"), 2)
+    keep_ref[...] = both[part]
+    send_ref[...] = both[1 - part].astype(BF16)
 
 
 def query_grad_kernel(ds_ref, kt_ref, o0, o1, o2, o3, all_ref):
@@ -136,12 +171,6 @@
         o[...] = all_ref[jnp.bitwise_xor(me, by)]
 
 
-def pair_kernel(keep_ref, key_ref, value_ref, out_ref):
-    w = key_ref.shape[-1]
-    out_ref[:, :, :w] = (keep_ref[:, :, :w].astype(F32) + key_ref[...].astype(F32)).astype(BF16)
-    out_ref[:, :, w:] = (keep_ref[:, :, w:].astype(F32) + value_ref[...].astype(F32)).astype(BF16)
-
-
 def project_kernel(a_ref, b_ref, c_ref, d_ref, w_ref, o0, o1, o2, o3, all_ref):
     total = sum(r[...].astype(F32) for r in (a_ref, b_ref, c_ref, d_ref)).astype(BF16)
     tile = w_ref.shape[0] // W_TILES
@@ -155,14 +184,12 @@
         o[...] = all_ref[lax.rem(me + by, 4)]
 
 
-def finish_kernel(kv_ref, a_ref, b_ref, c_ref, d_ref, key_ref, value_ref, input_ref):
-    total = kv_ref[0].astype(F32)
-    for k in range(1, kv_ref.shape[0]):
-        total += kv_ref[k].astype(F32)
+def finish_kernel(keep_ref, got_ref, a_ref, b_ref, c_ref, d_ref, key_ref, value_ref, input_ref):
+    total = keep_ref[...] + got_ref[...].astype(F32)
     width = key_ref.shape[1]
     key_ref[...] = total[:, :width]
     value_ref[...] = total[:, width:]
-    input_ref[...] = sum(r[...].astype(F32) for r in (a_ref, b_ref, c_ref, d_ref)).astype(BF16)
+    input_ref[...] = added(a_ref[...], b_ref[...], c_ref[...], d_ref[...])
 
 
 def moved(x, axis, to):
@@ -191,49 +218,64 @@
     heads = q.shape[1] // HD
     d_model = w.shape[0]
     on = pltpu.VMEM
-    e, dp, kt, stat, q, d = call(
+    e, dp, kt, stat, q, d, w = call(
         local_kernel,
         [on((heads, keys, ROWS), F32), on((heads, keys, ROWS), F32), on((width, keys), BF16),
-         on((24, ROWS), F32), on(q.shape, BF16), on(d.shape, BF16)],
+         on((24, ROWS), F32), on(q.shape, BF16), on(d.shape, BF16), on(w.shape, BF16)],
         [pltpu.with_memory_space_constraint(x, pltpu.HBM)
-         for x in (key_exps.T, value_exps.T, q, d, key_codes, value_codes)],
+         for x in (key_exps.T, value_exps.T, q, d, key_codes, value_codes, w)],
         scratch=[on(key_codes.shape, jnp.int32), on(key_codes.shape, jnp.int32),
                  on(key_codes.shape, BF16), on(key_codes.shape, BF16),
                  pltpu.SMEM(key_exps.shape[::-1], jnp.int32), pltpu.SMEM(key_exps.shape[::-1], jnp.int32),
-                 pltpu.SemaphoreType.DMA((6,))],
-        limit=16, specs=[HBM] * 6,
+                 pltpu.SemaphoreType.DMA((7,))],
+        limit=16, specs=[HBM] * 7,
     )
     stats = [stat] + [moved(stat, "key", lambda i: i ^ by) for by in (1, 2, 3)]
     slab = keys // DEPTH
-    half = (DEPTH // 2, slab, width)
-    ds, keep, send_v, send_k = call(
+    rows = ROWS // 4
+    ds, kv, far_k, far_v = call(
         cache_grad_kernel,
-        [on((heads, keys, ROWS), BF16), on((*half[:2], 2 * width), BF16), on(half, BF16), on(half, BF16)],
+        [on((heads, keys, ROWS), BF16), on((DEPTH, slab, 2 * width), BF16),
+         on((slab, width), BF16), on((slab, width), BF16)],
         (*stats, e, dp, q, d),
-        scratch=[on((2, *half[:2], 2 * width), BF16)],
-    )
-    got_v = moved(send_v, "section", lambda i: deeper(i, 1 - 2 * (i // 2 % 2)))
-    got_k = moved(send_k, "section", lambda i: deeper(i, 2 * (i // 2 % 2) - 1))
-    rows = ROWS // 4
+    )
+    down = moved(far_k, "section", lambda i: deeper(i, -1))
+    up = moved(far_v, "section", lambda i: deeper(i, 1))
     parts = call(
         query_grad_kernel,
         [on((rows, heads * HD), BF16)] * 4, (ds, kt),
         scratch=[on((4, rows, heads * HD), BF16)],
     )
-    keep, parts = lax.optimization_barrier((keep, parts))
+    kv, parts = lax.optimization_barrier((kv, parts))
     parts = [parts[0]] + [moved(parts[by], "key", lambda i: i ^ by) for by in (1, 2, 3)]
-    (kv,) = call(pair_kernel, [jax.ShapeDtypeStruct((*half[:2], 2 * width), BF16)], (keep, got_k, got_v))
-    groups = [[(2 * a + p) * 2 + xh for a in range(DEPTH // 2) for xh in range(2)] for p in range(2)]
-    kv = lax.all_to_all(kv.reshape(DEPTH, slab // 2, 2 * width), "section", 0, 0, axis_index_groups=groups, tiled=True)
+    whole = on((slab, 2 * width), BF16)
+    up, down = call(join_far_kernel, [whole] * 2, (kv, up, down))
+    down = moved(down, "section", lambda i: deeper(i, -1))
+    up = moved(up, "section", lambda i: deeper(i, 1))
+    up, down = call(functools.partial(join_kernel, 2), [whole] * 2, (kv, up, down))
+    down = moved(down, "section", lambda i: deeper(i, -1))
+    up = moved(up, "section", lambda i: deeper(i, 1))
     parts = call(
-        project_kernel, [on((rows // 4, d_model), BF16)] * 4, (*parts, w), scratch=[on((4, rows // 4, d_model), BF16)]
-    )
+        project_kernel,
+        [on((rows // 4, d_model), BF16)] * 4, (*parts, w),
+        scratch=[on((4, rows // 4, d_model), BF16)],
+    )
+    kv, parts = lax.optimization_barrier((kv, parts))
+    up, down = call(functools.partial(join_kernel, 1), [whole] * 2, (kv, up, down))
+    down = moved(down, "section", lambda i: deeper(i, -1))
+    up = moved(up, "section", lambda i: deeper(i, 1))
     parts = [parts[0]] + [moved(parts[by], "head", lambda i: (i + by) % 4) for by in (1, 2, 3)]
+    keep, send = call(
+        last_join_kernel,
+        [on((slab // 2, 2 * width), F32), on((slab // 2, 2 * width), BF16)], (kv, up, down),
+        scratch=[on((2, slab // 2, 2 * width), F32)],
+    )
+    got = moved(send, "section", lambda i: i ^ 1)
     key_grad, value_grad, input_grad = call(
         finish_kernel,
         [jax.ShapeDtypeStruct((slab // 2, width), F32), jax.ShapeDtypeStruct((slab // 2, width), F32),
          jax.ShapeDtypeStruct((rows // 4, d_model), BF16)],
-        (kv, *parts),
+        (keep, got, *parts),
     )
     return input_grad[None], key_grad, value_grad
 

time: 57.6 us -> 53.8 us (0.934)
  waiting for transfers between devices: 22.6 us -> 15.2 us
  starting transfers between devices: 21 us -> 27.8 us
  local copies, waits for them, and re-layouts: 2.34 us -> 0 us
  Pallas kernels: 10.1 us -> 9.27 us
    ppermute x11 -> x18, starting transfers between devices: 14.8 us -> 27.8 us  [moved(): lax.ppermute(x, axis, [(i, to(i)) for i in range(lax.axis_size(axis))])]
    ppermute x11 -> x18, waiting for transfers between devices: 22.6 us -> 15.2 us  [moved(): lax.ppermute(x, axis, [(i, to(i)) for i in range(lax.axis_size(axis))])]
    all_to_all x1 -> x0, starting transfers between devices: 6.27 us -> none  [step(): lax.all_to_all(kv.reshape(DEPTH, slab // 2, 2 * width), 'section', 0, 0,...]
    unnamed x2 -> x0, local copies, waits for them, and re-layouts: 2.34 us -> none
    pallas_call x6 -> x9, Pallas kernels: 10.1 us -> 9.27 us  [call(): pl.pallas_call(kernel, in_specs=specs or [VMEM] * len(ins), out_specs=[VM...]
  transfers between devices with their start and end apart: 12 -> 18, of which waited for: 8 -> 9; matrix products, arithmetic and copies ran while one was open for 0% -> 0% of each run, Pallas kernels for 4% -> 4%
where the time goes in v1:
time: 53.8 us; the launch traced here: 53.1 us
  starting transfers between devices  27.8 us (52%)
  waiting for transfers between devices  15.2 us (28%)
  Pallas kernels  9.27 us (17%)
  between operations  0.73 us (1%)
    ppermute x18, starting transfers between devices, moved(): lax.ppermute(x, axis, [(i, to(i)) for i in range(lax.axis_size(axis))])  27.8 us
    ppermute x18, waiting for transfers between devices, moved(): lax.ppermute(x, axis, [(i, to(i)) for i in range(lax.axis_size(axis))])  15.2 us
    pallas_call x9, Pallas kernels, call(): pl.pallas_call(kernel, in_specs=specs or [VMEM] * len(ins), out_specs=[VM...  9.27 us
  transfers between devices with their start and end apart: 18, of which 9 were waited for; matrix products, arithmetic and copies ran while one was open for 0% of the time, Pallas kernels for 4%

profile of v1, /device:TPU:8, one launch (start us, length us, event | category | flops | bytes accessed | tf_op | source)
XLA Modules:
  0.0 53.1 jit_solution(14596097121198483863)
XLA Ops:
  0.6 4.2 %shard_map.94 = (f32[6,1024,256]{2,1,0:T(8,128)S(1)}, f32[6,1024,256]{2,1,0:T(8,128)S(1)}, bf16[256,1024]{1,0:T(8,128)(2,1)S(1)}, f32[24,256]{1,0:T(8,128)S(1)},...) custom-call(s32[2,16]{1,0:T(2,128)} %bitcast.9, s32[2,16]{1,0:T(2,128)} %bitcast.10, ...), custom_call_target="tpu_custom_call" | custom-call | flops 268435456 | bytes 1048576 | tf_op jit(solution)/shard_map/pallas_call | solution.py:204
  4.8 1.0 %collective-permute-start.2 = (f32[24,256]{1,0:T(8,128)S(1)}, f32[24,256]{1,0:T(8,128)S(1)}, u32[]{:S(2)}, u32[]{:S(2)}) collective-permute-start(f32[24,256]{1,0:T(8,128)S(1)} %get-tuple-element.43.refs_0_), channel_id=1, source_target_pairs={{0,3},{1,2},{2,1},{3,0},{4,7},{5,6},{6,5},{7,4},{8,11},{9,10},{10,... | collective-permute-start | bytes 73736 | tf_op jit(solution)/shard_map/ppermute | solution.py:196
  6.8 1.6 %collective-permute-done.2.refs_3_ = f32[24,256]{1,0:T(8,128)S(1)} collective-permute-done((f32[24,256]{1,0:T(8,128)S(1)}, f32[24,256]{1,0:T(8,128)S(1)}, u32[]{:S(2)}, u32[]{:S(2)}) %collective-permute-start.2) | collective-permute-done | bytes 24608 | tf_op jit(solution)/shard_map/ppermute | solution.py:196
  8.4 1.3 %collective-permute-done.1.refs_2_ = f32[24,256]{1,0:T(8,128)S(1)} collective-permute-done((f32[24,256]{1,0:T(8,128)S(1)}, f32[24,256]{1,0:T(8,128)S(1)}, u32[]{:S(2)}, u32[]{:S(2)}) %collective-permute-start.1) | collective-permute-done | bytes 24608 | tf_op jit(solution)/shard_map/ppermute | solution.py:196
  9.7 1.9 %shard_map.95 = (bf16[6,1024,256]{2,1,0:T(8,128)(2,1)S(1)}, bf16[8,128,512]{2,1,0:T(8,128)(2,1)S(1)}, bf16[128,256]{1,0:T(8,128)(2,1)S(1)}, bf16[128,256]{1,0:T(8,128)(2,1)S(1)}) custom-call(f32[24,256]{1,0:T(8,128)S(1)} %get-tuple-element.43.refs_0_, f32[24,256]{1,0:T(8,128)S(1)} %collective-permute-done.refs_1_, ...), custom_call_target="tpu_custom_call" | custom-call | flops 268435456 | bytes 1048576 | tf_op jit(solution)/shard_map/pallas_call | solution.py:204
  11.5 2.0 %collective-permute-start.6 = (bf16[128,256]{1,0:T(8,128)(2,1)S(1)}, bf16[128,256]{1,0:T(8,128)(2,1)S(1)}, u32[]{:S(2)}, u32[]{:S(2)}) collective-permute-start(bf16[128,256]{1,0:T(8,128)(2,1)S(1)} %get-tuple-element.66), channel_id=1, source_target_pairs={{0,32},{16,48},{32,64},{48,80},{64,96},{80,112},{96,128},{112,144}... | collective-permute-start | bytes 196616 | tf_op jit(solution)/shard_map/ppermute | solution.py:196
  13.5 4.0 %collective-permute-start.7 = (bf16[128,256]{1,0:T(8,128)(2,1)S(1)}, bf16[128,256]{1,0:T(8,128)(2,1)S(1)}, u32[]{:S(2)}, u32[]{:S(2)}) collective-permute-start(bf16[128,256]{1,0:T(8,128)(2,1)S(1)} %get-tuple-element.67), channel_id=1, source_target_pairs={{0,224},{16,240},{32,0},{48,16},{64,32},{80,48},{96,64},{112,80},{... | collective-permute-start | bytes 196616 | tf_op jit(solution)/shard_map/ppermute | solution.py:196
  18.3 1.4 %collective-permute-done.6.up_ref = bf16[128,256]{1,0:T(8,128)(2,1)S(1)} collective-permute-done((bf16[128,256]{1,0:T(8,128)(2,1)S(1)}, bf16[128,256]{1,0:T(8,128)(2,1)S(1)}, u32[]{:S(2)}, u32[]{:S(2)}) %collective-permute-start.6) | collective-permute-done | bytes 65568 | tf_op jit(solution)/shard_map/ppermute | solution.py:196
  19.9 3.4 %collective-permute-start.9 = (bf16[128,512]{1,0:T(8,128)(2,1)S(1)}, bf16[128,512]{1,0:T(8,128)(2,1)S(1)}, u32[]{:S(2)}, u32[]{:S(2)}) collective-permute-start(bf16[128,512]{1,0:T(8,128)(2,1)S(1)} %get-tuple-element.69), channel_id=1, source_target_pairs={{0,224},{16,240},{32,0},{48,16},{64,32},{80,48},{96,64},{112,80},{... | collective-permute-start | bytes 393224 | tf_op jit(solution)/shard_map/ppermute | solution.py:196
  23.2 2.9 %collective-permute-done.8.up_ref = bf16[128,512]{1,0:T(8,128)(2,1)S(1)} collective-permute-done((bf16[128,512]{1,0:T(8,128)(2,1)S(1)}, bf16[128,512]{1,0:T(8,128)(2,1)S(1)}, u32[]{:S(2)}, u32[]{:S(2)}) %collective-permute-start.8) | collective-permute-done | bytes 131104 | tf_op jit(solution)/shard_map/ppermute | solution.py:196
  26.2 3.0 %collective-permute-start.10 = (bf16[128,512]{1,0:T(8,128)(2,1)S(1)}, bf16[128,512]{1,0:T(8,128)(2,1)S(1)}, u32[]{:S(2)}, u32[]{:S(2)}) collective-permute-start(bf16[128,512]{1,0:T(8,128)(2,1)S(1)} %get-tuple-element.70), channel_id=1, source_target_pairs={{0,32},{16,48},{32,64},{48,80},{64,96},{80,112},{96,128},{112,144}... | collective-permute-start | bytes 393224 | tf_op jit(solution)/shard_map/ppermute | solution.py:196
  29.7 0.8 %collective-permute-start.4 = (bf16[64,768]{1,0:T(8,128)(2,1)S(1)}, bf16[64,768]{1,0:T(8,128)(2,1)S(1)}, u32[]{:S(2)}, u32[]{:S(2)}) collective-permute-start(bf16[64,768]{1,0:T(8,128)(2,1)S(1)} %get-tuple-element.58), channel_id=1, source_target_pairs={{0,2},{1,3},{2,0},{3,1},{4,6},{5,7},{6,4},{7,5},{8,10},{9,11},{10,... | collective-permute-start | bytes 294920 | tf_op jit(solution)/shard_map/ppermute | solution.py:196
  30.4 1.1 %collective-permute-start.5 = (bf16[64,768]{1,0:T(8,128)(2,1)S(1)}, bf16[64,768]{1,0:T(8,128)(2,1)S(1)}, u32[]{:S(2)}, u32[]{:S(2)}) collective-permute-start(bf16[64,768]{1,0:T(8,128)(2,1)S(1)} %get-tuple-element.59), channel_id=1, source_target_pairs={{0,3},{1,2},{2,1},{3,0},{4,7},{5,6},{6,5},{7,4},{8,11},{9,10},{10,... | collective-permute-start | bytes 294920 | tf_op jit(solution)/shard_map/ppermute | solution.py:196
  31.5 3.8 %collective-permute-done.4.c_ref = bf16[64,768]{1,0:T(8,128)(2,1)S(1)} collective-permute-done((bf16[64,768]{1,0:T(8,128)(2,1)S(1)}, bf16[64,768]{1,0:T(8,128)(2,1)S(1)}, u32[]{:S(2)}, u32[]{:S(2)}) %collective-permute-start.4) | collective-permute-done | bytes 98336 | tf_op jit(solution)/shard_map/ppermute | solution.py:196
  35.3 1.2 %collective-permute-done.5.d_ref = bf16[64,768]{1,0:T(8,128)(2,1)S(1)} collective-permute-done((bf16[64,768]{1,0:T(8,128)(2,1)S(1)}, bf16[64,768]{1,0:T(8,128)(2,1)S(1)}, u32[]{:S(2)}, u32[]{:S(2)}) %collective-permute-start.5) | collective-permute-done | bytes 98336 | tf_op jit(solution)/shard_map/ppermute | solution.py:196
  36.5 1.5 %shard_map.97 = (bf16[16,3072]{1,0:T(8,128)(2,1)S(1)}, bf16[16,3072]{1,0:T(8,128)(2,1)S(1)}, bf16[16,3072]{1,0:T(8,128)(2,1)S(1)}, bf16[16,3072]{1,0:T(8,128)(2,1)S(1)}) custom-call(bf16[64,768]{1,0:T(8,128)(2,1)S(1)} %get-tuple-element.56.a_ref, bf16[64,768]{1,0:T(8,128)(2,1)S(1)} %collective-permute-done.3.b_ref, ...), custom_call_target="tpu_custom_call" | custom-call | flops 268435456 | bytes 1048576 | tf_op jit(solution)/shard_map/pallas_call | solution.py:204
  38.2 1.6 %collective-permute-start.12 = (bf16[128,512]{1,0:T(8,128)(2,1)S(1)}, bf16[128,512]{1,0:T(8,128)(2,1)S(1)}, u32[]{:S(2)}, u32[]{:S(2)}) collective-permute-start(bf16[128,512]{1,0:T(8,128)(2,1)S(1)} %get-tuple-element.72), channel_id=1, source_target_pairs={{0,32},{16,48},{32,64},{48,80},{64,96},{80,112},{96,128},{112,144}... | collective-permute-start | bytes 393224 | tf_op jit(solution)/shard_map/ppermute | solution.py:196
  39.8 1.7 %collective-permute-start.13 = (bf16[128,512]{1,0:T(8,128)(2,1)S(1)}, bf16[128,512]{1,0:T(8,128)(2,1)S(1)}, u32[]{:S(2)}, u32[]{:S(2)}) collective-permute-start(bf16[128,512]{1,0:T(8,128)(2,1)S(1)} %get-tuple-element.73), channel_id=1, source_target_pairs={{0,224},{16,240},{32,0},{48,16},{64,32},{80,48},{96,64},{112,80},{... | collective-permute-start | bytes 393224 | tf_op jit(solution)/shard_map/ppermute | solution.py:196
  41.5 1.6 %collective-permute-start.15 = (bf16[16,3072]{1,0:T(8,128)(2,1)S(1)}, bf16[16,3072]{1,0:T(8,128)(2,1)S(1)}, u32[]{:S(2)}, u32[]{:S(2)}) collective-permute-start(bf16[16,3072]{1,0:T(8,128)(2,1)S(1)} %get-tuple-element.77), channel_id=1, source_target_pairs={{0,4},{4,8},{8,12},{12,0},{1,5},{5,9},{9,13},{13,1},{2,6},{6,10},{... | collective-permute-start | bytes 294920 | tf_op jit(solution)/shard_map/ppermute | solution.py:196
  43.1 0.9 %collective-permute-start.16 = (bf16[16,3072]{1,0:T(8,128)(2,1)S(1)}, bf16[16,3072]{1,0:T(8,128)(2,1)S(1)}, u32[]{:S(2)}, u32[]{:S(2)}) collective-permute-start(bf16[16,3072]{1,0:T(8,128)(2,1)S(1)} %get-tuple-element.78), channel_id=1, source_target_pairs={{0,8},{4,12},{8,0},{12,4},{1,9},{5,13},{9,1},{13,5},{2,10},{6,14},... | collective-permute-start | bytes 294920 | tf_op jit(solution)/shard_map/ppermute | solution.py:196
  44.0 2.4 %collective-permute-start.17 = (bf16[16,3072]{1,0:T(8,128)(2,1)S(1)}, bf16[16,3072]{1,0:T(8,128)(2,1)S(1)}, u32[]{:S(2)}, u32[]{:S(2)}) collective-permute-start(bf16[16,3072]{1,0:T(8,128)(2,1)S(1)} %get-tuple-element.79), channel_id=1, source_target_pairs={{0,12},{4,0},{8,4},{12,8},{1,13},{5,1},{9,5},{13,9},{2,14},{6,2},{... | collective-permute-start | bytes 294920 | tf_op jit(solution)/shard_map/ppermute | solution.py:196
  46.5 2.8 %collective-permute-start.14 = (bf16[64,512]{1,0:T(8,128)(2,1)S(1)}, bf16[64,512]{1,0:T(8,128)(2,1)S(1)}, u32[]{:S(2)}, u32[]{:S(2)}) collective-permute-start(bf16[64,512]{1,0:T(8,128)(2,1)S(1)} %get-tuple-element.75), channel_id=1, source_target_pairs={{0,16},{16,0},{32,48},{48,32},{64,80},{80,64},{96,112},{112,96},{1... | collective-permute-start | bytes 196616 | tf_op jit(solution)/shard_map/ppermute | solution.py:196
  50.0 2.3 %collective-permute-done.14.got_ref = bf16[64,512]{1,0:T(8,128)(2,1)S(1)} collective-permute-done((bf16[64,512]{1,0:T(8,128)(2,1)S(1)}, bf16[64,512]{1,0:T(8,128)(2,1)S(1)}, u32[]{:S(2)}, u32[]{:S(2)}) %collective-permute-start.14) | collective-permute-done | bytes 65568 | tf_op jit(solution)/shard_map/ppermute | solution.py:196
  52.4 0.7 %shard_map.102 = (f32[64,256]{1,0:T(8,128)}, f32[64,256]{1,0:T(8,128)}, bf16[16,3072]{1,0:T(8,128)(2,1)}) custom-call(f32[64,512]{1,0:T(8,128)S(1)} %get-tuple-element.74.keep_ref, bf16[64,512]{1,0:T(8,128)(2,1)S(1)} %collective-permute-done.14.got_ref, bf16[16,3072]{1,0:T(8,128)(2,1)S(1)} %get-tuple-element.76.a_ref, ...), custom_call_target="tpu_custom_call" | custom-call | flops 268435456 | bytes 1048576 | tf_op jit(solution)/shard_map/pallas_call | solution.py:204
  (21 shorter events, 3.2 us)
Async XLA Ops:
  4.8 3.6 %collective-permute-start.2 = (f32[24,256]{1,0:T(8,128)S(1)}, f32[24,256]{1,0:T(8,128)S(1)}, u32[]{:S(2)}, u32[]{:S(2)}) collective-permute-start(f32[24,256]{1,0:T(8,128)S(1)} %get-tuple-element.43.refs_0_), channel_id=1, source_target_pairs={{0,3},{1,2},{2,1},{3,0},{4,7},{5,6},{6,5},{7,4},{8,11},{9,10},{10,... | collective-permute-start | bytes 73736 | tf_op jit(solution)/shard_map/ppermute | solution.py:196
  5.8 3.8 %collective-permute-start.1 = (f32[24,256]{1,0:T(8,128)S(1)}, f32[24,256]{1,0:T(8,128)S(1)}, u32[]{:S(2)}, u32[]{:S(2)}) collective-permute-start(f32[24,256]{1,0:T(8,128)S(1)} %get-tuple-element.43.refs_0_), channel_id=1, source_target_pairs={{0,2},{1,3},{2,0},{3,1},{4,6},{5,7},{6,4},{7,5},{8,10},{9,11},{10,... | collective-permute-start | bytes 73736 | tf_op jit(solution)/shard_map/ppermute | solution.py:196
  6.5 3.2 %collective-permute-start = (f32[24,256]{1,0:T(8,128)S(1)}, f32[24,256]{1,0:T(8,128)S(1)}, u32[]{:S(2)}, u32[]{:S(2)}) collective-permute-start(f32[24,256]{1,0:T(8,128)S(1)} %get-tuple-element.43.refs_0_), channel_id=1, source_target_pairs={{0,1},{1,0},{2,3},{3,2},{4,5},{5,4},{6,7},{7,6},{8,9},{9,8},{10,11... | collective-permute-start | bytes 73736 | tf_op jit(solution)/shard_map/ppermute | solution.py:196
  11.5 8.2 %collective-permute-start.6 = (bf16[128,256]{1,0:T(8,128)(2,1)S(1)}, bf16[128,256]{1,0:T(8,128)(2,1)S(1)}, u32[]{:S(2)}, u32[]{:S(2)}) collective-permute-start(bf16[128,256]{1,0:T(8,128)(2,1)S(1)} %get-tuple-element.66), channel_id=1, source_target_pairs={{0,32},{16,48},{32,64},{48,80},{64,96},{80,112},{96,128},{112,144}... | collective-permute-start | bytes 196616 | tf_op jit(solution)/shard_map/ppermute | solution.py:196
  13.5 6.2 %collective-permute-start.7 = (bf16[128,256]{1,0:T(8,128)(2,1)S(1)}, bf16[128,256]{1,0:T(8,128)(2,1)S(1)}, u32[]{:S(2)}, u32[]{:S(2)}) collective-permute-start(bf16[128,256]{1,0:T(8,128)(2,1)S(1)} %get-tuple-element.67), channel_id=1, source_target_pairs={{0,224},{16,240},{32,0},{48,16},{64,32},{80,48},{96,64},{112,80},{... | collective-permute-start | bytes 196616 | tf_op jit(solution)/shard_map/ppermute | solution.py:196
  19.8 6.3 %collective-permute-start.8 = (bf16[128,512]{1,0:T(8,128)(2,1)S(1)}, bf16[128,512]{1,0:T(8,128)(2,1)S(1)}, u32[]{:S(2)}, u32[]{:S(2)}) collective-permute-start(bf16[128,512]{1,0:T(8,128)(2,1)S(1)} %get-tuple-element.68), channel_id=1, source_target_pairs={{0,32},{16,48},{32,64},{48,80},{64,96},{80,112},{96,128},{112,144}... | collective-permute-start | bytes 393224 | tf_op jit(solution)/shard_map/ppermute | solution.py:196
  19.9 6.2 %collective-permute-start.9 = (bf16[128,512]{1,0:T(8,128)(2,1)S(1)}, bf16[128,512]{1,0:T(8,128)(2,1)S(1)}, u32[]{:S(2)}, u32[]{:S(2)}) collective-permute-start(bf16[128,512]{1,0:T(8,128)(2,1)S(1)} %get-tuple-element.69), channel_id=1, source_target_pairs={{0,224},{16,240},{32,0},{48,16},{64,32},{80,48},{96,64},{112,80},{... | collective-permute-start | bytes 393224 | tf_op jit(solution)/shard_map/ppermute | solution.py:196
  26.2 11.9 %collective-permute-start.10 = (bf16[128,512]{1,0:T(8,128)(2,1)S(1)}, bf16[128,512]{1,0:T(8,128)(2,1)S(1)}, u32[]{:S(2)}, u32[]{:S(2)}) collective-permute-start(bf16[128,512]{1,0:T(8,128)(2,1)S(1)} %get-tuple-element.70), channel_id=1, source_target_pairs={{0,32},{16,48},{32,64},{48,80},{64,96},{80,112},{96,128},{112,144}... | collective-permute-start | bytes 393224 | tf_op jit(solution)/shard_map/ppermute | solution.py:196
  29.2 8.9 %collective-permute-start.11 = (bf16[128,512]{1,0:T(8,128)(2,1)S(1)}, bf16[128,512]{1,0:T(8,128)(2,1)S(1)}, u32[]{:S(2)}, u32[]{:S(2)}) collective-permute-start(bf16[128,512]{1,0:T(8,128)(2,1)S(1)} %get-tuple-element.71), channel_id=1, source_target_pairs={{0,224},{16,240},{32,0},{48,16},{64,32},{80,48},{96,64},{112,80},{... | collective-permute-start | bytes 393224 | tf_op jit(solution)/shard_map/ppermute | solution.py:196
  29.7 1.9 %collective-permute-start.3 = (bf16[64,768]{1,0:T(8,128)(2,1)S(1)}, bf16[64,768]{1,0:T(8,128)(2,1)S(1)}, u32[]{:S(2)}, u32[]{:S(2)}) collective-permute-start(bf16[64,768]{1,0:T(8,128)(2,1)S(1)} %get-tuple-element.57), channel_id=1, source_target_pairs={{0,1},{1,0},{2,3},{3,2},{4,5},{5,4},{6,7},{7,6},{8,9},{9,8},{10,11... | collective-permute-start | bytes 294920 | tf_op jit(solution)/shard_map/ppermute | solution.py:196
  29.7 5.7 %collective-permute-start.4 = (bf16[64,768]{1,0:T(8,128)(2,1)S(1)}, bf16[64,768]{1,0:T(8,128)(2,1)S(1)}, u32[]{:S(2)}, u32[]{:S(2)}) collective-permute-start(bf16[64,768]{1,0:T(8,128)(2,1)S(1)} %get-tuple-element.58), channel_id=1, source_target_pairs={{0,2},{1,3},{2,0},{3,1},{4,6},{5,7},{6,4},{7,5},{8,10},{9,11},{10,... | collective-permute-start | bytes 294920 | tf_op jit(solution)/shard_map/ppermute | solution.py:196
  30.4 6.1 %collective-permute-start.5 = (bf16[64,768]{1,0:T(8,128)(2,1)S(1)}, bf16[64,768]{1,0:T(8,128)(2,1)S(1)}, u32[]{:S(2)}, u32[]{:S(2)}) collective-permute-start(bf16[64,768]{1,0:T(8,128)(2,1)S(1)} %get-tuple-element.59), channel_id=1, source_target_pairs={{0,3},{1,2},{2,1},{3,0},{4,7},{5,6},{6,5},{7,4},{8,11},{9,10},{10,... | collective-permute-start | bytes 294920 | tf_op jit(solution)/shard_map/ppermute | solution.py:196
  38.2 8.2 %collective-permute-start.12 = (bf16[128,512]{1,0:T(8,128)(2,1)S(1)}, bf16[128,512]{1,0:T(8,128)(2,1)S(1)}, u32[]{:S(2)}, u32[]{:S(2)}) collective-permute-start(bf16[128,512]{1,0:T(8,128)(2,1)S(1)} %get-tuple-element.72), channel_id=1, source_target_pairs={{0,32},{16,48},{32,64},{48,80},{64,96},{80,112},{96,128},{112,144}... | collective-permute-start | bytes 393224 | tf_op jit(solution)/shard_map/ppermute | solution.py:196
  39.8 6.6 %collective-permute-start.13 = (bf16[128,512]{1,0:T(8,128)(2,1)S(1)}, bf16[128,512]{1,0:T(8,128)(2,1)S(1)}, u32[]{:S(2)}, u32[]{:S(2)}) collective-permute-start(bf16[128,512]{1,0:T(8,128)(2,1)S(1)} %get-tuple-element.73), channel_id=1, source_target_pairs={{0,224},{16,240},{32,0},{48,16},{64,32},{80,48},{96,64},{112,80},{... | collective-permute-start | bytes 393224 | tf_op jit(solution)/shard_map/ppermute | solution.py:196
  41.5 7.8 %collective-permute-start.15 = (bf16[16,3072]{1,0:T(8,128)(2,1)S(1)}, bf16[16,3072]{1,0:T(8,128)(2,1)S(1)}, u32[]{:S(2)}, u32[]{:S(2)}) collective-permute-start(bf16[16,3072]{1,0:T(8,128)(2,1)S(1)} %get-tuple-element.77), channel_id=1, source_target_pairs={{0,4},{4,8},{8,12},{12,0},{1,5},{5,9},{9,13},{13,1},{2,6},{6,10},{... | collective-permute-start | bytes 294920 | tf_op jit(solution)/shard_map/ppermute | solution.py:196
  43.1 6.7 %collective-permute-start.16 = (bf16[16,3072]{1,0:T(8,128)(2,1)S(1)}, bf16[16,3072]{1,0:T(8,128)(2,1)S(1)}, u32[]{:S(2)}, u32[]{:S(2)}) collective-permute-start(bf16[16,3072]{1,0:T(8,128)(2,1)S(1)} %get-tuple-element.78), channel_id=1, source_target_pairs={{0,8},{4,12},{8,0},{12,4},{1,9},{5,13},{9,1},{13,5},{2,10},{6,14},... | collective-permute-start | bytes 294920 | tf_op jit(solution)/shard_map/ppermute | solution.py:196
  44.0 6.0 %collective-permute-start.17 = (bf16[16,3072]{1,0:T(8,128)(2,1)S(1)}, bf16[16,3072]{1,0:T(8,128)(2,1)S(1)}, u32[]{:S(2)}, u32[]{:S(2)}) collective-permute-start(bf16[16,3072]{1,0:T(8,128)(2,1)S(1)} %get-tuple-element.79), channel_id=1, source_target_pairs={{0,12},{4,0},{8,4},{12,8},{1,13},{5,1},{9,5},{13,9},{2,14},{6,2},{... | collective-permute-start | bytes 294920 | tf_op jit(solution)/shard_map/ppermute | solution.py:196
  46.5 5.9 %collective-permute-start.14 = (bf16[64,512]{1,0:T(8,128)(2,1)S(1)}, bf16[64,512]{1,0:T(8,128)(2,1)S(1)}, u32[]{:S(2)}, u32[]{:S(2)}) collective-permute-start(bf16[64,512]{1,0:T(8,128)(2,1)S(1)} %get-tuple-element.75), channel_id=1, source_target_pairs={{0,16},{16,0},{32,48},{48,32},{64,80},{80,64},{96,112},{112,96},{1... | collective-permute-start | bytes 196616 | tf_op jit(solution)/shard_map/ppermute | solution.py:196

commit v2 on v1

--- a/solution.py
+++ b/solution.py
@@ -1,5 +1,3 @@
-import functools
-
 import jax
 import jax.numpy as jnp
 from jax import lax
@@ -93,7 +91,7 @@
 
 
 def cache_grad_kernel(*refs):
-    stats, (e_ref, dp_ref, q_ref, d_ref, ds_ref, kv_ref, far_k, far_v) = refs[:4], refs[4:]
+    stats, (e_ref, dp_ref, q_ref, d_ref, ds_ref, kv_ref, near_down, near_up, far_k, far_v) = refs[:4], refs[4:]
     top = stats[0][0:8, :]
     for s in stats[1:]:
         top = jnp.maximum(top, s[0:8, :])
@@ -120,6 +118,9 @@
             at = slice(z * slab, (z + 1) * slab)
             kv_ref[z, :, g * HD:(g + 1) * HD] = key_low[at, :]
             kv_ref[z, :, (2 + g) * HD:(3 + g) * HD] = value_low[at, :]
+    for n, by in enumerate((1, 3)):
+        near_down[n] = kv_ref[away(-by)]
+        near_up[n] = kv_ref[away(by)]
     far = away(DEPTH // 2)
     far_k[...] = kv_ref[far, :, :2 * HD]
     far_v[...] = kv_ref[far, :, 2 * HD:]
@@ -129,32 +130,29 @@
     return lax.rem(lax.axis_index("section") // 2 + (by + DEPTH), DEPTH)
 
 
-def added(*terms):
-    return sum(t.astype(F32) for t in terms).astype(BF16)
-
-
-def join_far_kernel(kv_ref, up_ref, down_ref, to_up, to_down):
-    w = up_ref.shape[1]
-    above, below = away(3), away(-3)
-    to_up[:, :w] = kv_ref[above, :, :w]
-    to_up[:, w:] = added(kv_ref[above, :, w:], up_ref[...])
-    to_down[:, :w] = added(kv_ref[below, :, :w], down_ref[...])
-    to_down[:, w:] = kv_ref[below, :, w:]
-
-
-def join_kernel(by, kv_ref, up_ref, down_ref, to_up, to_down):
-    to_up[...] = added(kv_ref[away(by)], up_ref[...])
-    to_down[...] = added(kv_ref[away(-by)], down_ref[...])
-
-
-def last_join_kernel(kv_ref, up_ref, down_ref, keep_ref, send_ref, both):
-    rows = keep_ref.shape[0]
-    mine = kv_ref[away(0)].astype(F32) + up_ref[...].astype(F32) + down_ref[...].astype(F32)
-    both[0] = mine[:rows]
-    both[1] = mine[rows:]
+def total_of(*terms):
+    return sum(t.astype(F32) for t in terms)
+
+
+def collect_kernel(kv_ref, above_ref, below_ref, far_k, far_v,
+                   down_same, down_other, up_same, up_other, keep_ref, mine_other, both):
+    rows, w = keep_ref.shape[0], far_k.shape[1]
     part = lax.rem(lax.axis_index("section"), 2)
+    mine = total_of(kv_ref[away(0)], above_ref[0], below_ref[0])
+    for xh in range(2):
+        both[xh] = mine[xh * rows:(xh + 1) * rows, :]
     keep_ref[...] = both[part]
-    send_ref[...] = both[1 - part].astype(BF16)
+    mine_other[...] = both[1 - part].astype(BF16)
+    for by, near, far, cols, same, other in (
+        (-2, above_ref, far_k, slice(0, w), down_same, down_other),
+        (2, below_ref, far_v, slice(w, 2 * w), up_same, up_other),
+    ):
+        whole = total_of(kv_ref[away(by)], near[1])
+        for xh in range(2):
+            both[xh] = whole[xh * rows:(xh + 1) * rows, :]
+            both[xh, :, cols] += far[xh * rows:(xh + 1) * rows, :].astype(F32)
+        same[...] = both[part].astype(BF16)
+        other[...] = both[1 - part].astype(BF16)
 
 
 def query_grad_kernel(ds_ref, kt_ref, o0, o1, o2, o3, all_ref):
@@ -184,20 +182,21 @@
         o[...] = all_ref[lax.rem(me + by, 4)]
 
 
-def finish_kernel(keep_ref, got_ref, a_ref, b_ref, c_ref, d_ref, key_ref, value_ref, input_ref):
-    total = keep_ref[...] + got_ref[...].astype(F32)
+def finish_kernel(keep_ref, *refs):
+    got, parts, (key_ref, value_ref, input_ref) = refs[:5], refs[5:9], refs[9:]
+    total = total_of(keep_ref[...], *(r[...] for r in got))
     width = key_ref.shape[1]
     key_ref[...] = total[:, :width]
     value_ref[...] = total[:, width:]
-    input_ref[...] = added(a_ref[...], b_ref[...], c_ref[...], d_ref[...])
+    input_ref[...] = total_of(*(r[...] for r in parts)).astype(BF16)
 
 
 def moved(x, axis, to):
     return lax.ppermute(x, axis, [(i, to(i)) for i in range(lax.axis_size(axis))])
 
 
-def deeper(section, by):
-    return (section // 2 + by) % DEPTH * 2 + section % 2
+def deeper(by, across=0):
+    return lambda section: (section // 2 + by) % DEPTH * 2 + (section % 2 ^ across)
 
 
 def call(kernel, outs, ins, scratch=(), limit=16, specs=None, cost=1 << 28):
@@ -233,49 +232,49 @@
     stats = [stat] + [moved(stat, "key", lambda i: i ^ by) for by in (1, 2, 3)]
     slab = keys // DEPTH
     rows = ROWS // 4
-    ds, kv, far_k, far_v = call(
+    near = on((2, slab, 2 * width), BF16)
+    ds, kv, near_down, near_up, far_k, far_v = call(
         cache_grad_kernel,
         [on((heads, keys, ROWS), BF16), on((DEPTH, slab, 2 * width), BF16),
-         on((slab, width), BF16), on((slab, width), BF16)],
+         near, near, on((slab, width), BF16), on((slab, width), BF16)],
         (*stats, e, dp, q, d),
     )
-    down = moved(far_k, "section", lambda i: deeper(i, -1))
-    up = moved(far_v, "section", lambda i: deeper(i, 1))
+    above = moved(near_down, "section", deeper(-1))
+    below = moved(near_up, "section", deeper(1))
+    far_k = moved(far_k, "section", deeper(-2))
+    far_v = moved(far_v, "section", deeper(2))
     parts = call(
         query_grad_kernel,
         [on((rows, heads * HD), BF16)] * 4, (ds, kt),
         scratch=[on((4, rows, heads * HD), BF16)],
     )
-    kv, parts = lax.optimization_barrier((kv, parts))
     parts = [parts[0]] + [moved(parts[by], "key", lambda i: i ^ by) for by in (1, 2, 3)]
-    whole = on((slab, 2 * width), BF16)
-    up, down = call(join_far_kernel, [whole] * 2, (kv, up, down))
-    down = moved(down, "section", lambda i: deeper(i, -1))
-    up = moved(up, "section", lambda i: deeper(i, 1))
-    up, down = call(functools.partial(join_kernel, 2), [whole] * 2, (kv, up, down))
-    down = moved(down, "section", lambda i: deeper(i, -1))
-    up = moved(up, "section", lambda i: deeper(i, 1))
     parts = call(
         project_kernel,
         [on((rows // 4, d_model), BF16)] * 4, (*parts, w),
         scratch=[on((4, rows // 4, d_model), BF16)],
     )
     kv, parts = lax.optimization_barrier((kv, parts))
-    up, down = call(functools.partial(join_kernel, 1), [whole] * 2, (kv, up, down))
-    down = moved(down, "section", lambda i: deeper(i, -1))
-    up = moved(up, "section", lambda i: deeper(i, 1))
+    piece = on((slab // 2, 2 * width), BF16)
+    down_same, down_other, up_same, up_other, keep, mine_other = call(
+        collect_kernel,
+        [piece] * 4 + [on((slab // 2, 2 * width), F32), piece],
+        (kv, above, below, far_k, far_v),
+        scratch=[on((2, slab // 2, 2 * width), F32)],
+    )
+    got = [
+        moved(down_same, "section", deeper(-2)),
+        moved(up_same, "section", deeper(2)),
+        moved(down_other, "section", deeper(-2, 1)),
+        moved(up_other, "section", deeper(2, 1)),
+        moved(mine_other, "section", deeper(0, 1)),
+    ]
     parts = [parts[0]] + [moved(parts[by], "head", lambda i: (i + by) % 4) for by in (1, 2, 3)]
-    keep, send = call(
-        last_join_kernel,
-        [on((slab // 2, 2 * width), F32), on((slab // 2, 2 * width), BF16)], (kv, up, down),
-        scratch=[on((2, slab // 2, 2 * width), F32)],
-    )
-    got = moved(send, "section", lambda i: i ^ 1)
     key_grad, value_grad, input_grad = call(
         finish_kernel,
         [jax.ShapeDtypeStruct((slab // 2, width), F32), jax.ShapeDtypeStruct((slab // 2, width), F32),
          jax.ShapeDtypeStruct((rows // 4, d_model), BF16)],
-        (keep, got, *parts),
+        (keep, *got, *parts),
     )
     return input_grad[None], key_grad, value_grad
 

time: 53.8 us -> 52.2 us (0.970)
  the two profiles are of different devices: /device:TPU:8 before, /device:TPU:32 now
where the time goes in v2:
time: 52.2 us; the launch traced here: 52 us
  starting transfers between devices  31.6 us (61%)
  waiting for transfers between devices  10.5 us (20%)
  Pallas kernels  9.25 us (18%)
  between operations  0.69 us (1%)
    ppermute x18, starting transfers between devices, moved(): lax.ppermute(x, axis, [(i, to(i)) for i in range(lax.axis_size(axis))])  31.6 us
    ppermute x18, waiting for transfers between devices, moved(): lax.ppermute(x, axis, [(i, to(i)) for i in range(lax.axis_size(axis))])  10.5 us
    pallas_call x6, Pallas kernels, call(): pl.pallas_call(kernel, in_specs=specs or [VMEM] * len(ins), out_specs=[VM...  9.25 us
  transfers between devices with their start and end apart: 18, of which 4 were waited for; matrix products, arithmetic and copies ran while one was open for 0% of the time, Pallas kernels for 5%

profile of v2, /device:TPU:32, one launch (start us, length us, event | category | flops | bytes accessed | tf_op | source)
XLA Modules:
  0.0 52.0 jit_solution(1366717822344467186)
XLA Ops:
  0.6 4.2 %shard_map.94 = (f32[6,1024,256]{2,1,0:T(8,128)S(1)}, f32[6,1024,256]{2,1,0:T(8,128)S(1)}, bf16[256,1024]{1,0:T(8,128)(2,1)S(1)}, f32[24,256]{1,0:T(8,128)S(1)},...) custom-call(s32[2,16]{1,0:T(2,128)} %bitcast.9, s32[2,16]{1,0:T(2,128)} %bitcast.10, ...), custom_call_target="tpu_custom_call" | custom-call | flops 268435456 | bytes 1048576 | tf_op jit(solution)/shard_map/pallas_call | solution.py:203
  4.8 1.0 %collective-permute-start.2 = (f32[24,256]{1,0:T(8,128)S(1)}, f32[24,256]{1,0:T(8,128)S(1)}, u32[]{:S(2)}, u32[]{:S(2)}) collective-permute-start(f32[24,256]{1,0:T(8,128)S(1)} %get-tuple-element.38.refs_0_), channel_id=1, source_target_pairs={{0,3},{1,2},{2,1},{3,0},{4,7},{5,6},{6,5},{7,4},{8,11},{9,10},{10,... | collective-permute-start | bytes 73736 | tf_op jit(solution)/shard_map/ppermute | solution.py:195
  5.8 0.7 %collective-permute-start.1 = (f32[24,256]{1,0:T(8,128)S(1)}, f32[24,256]{1,0:T(8,128)S(1)}, u32[]{:S(2)}, u32[]{:S(2)}) collective-permute-start(f32[24,256]{1,0:T(8,128)S(1)} %get-tuple-element.38.refs_0_), channel_id=1, source_target_pairs={{0,2},{1,3},{2,0},{3,1},{4,6},{5,7},{6,4},{7,5},{8,10},{9,11},{10,... | collective-permute-start | bytes 73736 | tf_op jit(solution)/shard_map/ppermute | solution.py:195
  6.5 0.3 collective-permute-start
  6.8 1.6 %collective-permute-done.2.refs_3_ = f32[24,256]{1,0:T(8,128)S(1)} collective-permute-done((f32[24,256]{1,0:T(8,128)S(1)}, f32[24,256]{1,0:T(8,128)S(1)}, u32[]{:S(2)}, u32[]{:S(2)}) %collective-permute-start.2) | collective-permute-done | bytes 24608 | tf_op jit(solution)/shard_map/ppermute | solution.py:195
  8.4 1.3 %collective-permute-done.1.refs_2_ = f32[24,256]{1,0:T(8,128)S(1)} collective-permute-done((f32[24,256]{1,0:T(8,128)S(1)}, f32[24,256]{1,0:T(8,128)S(1)}, u32[]{:S(2)}, u32[]{:S(2)}) %collective-permute-start.1) | collective-permute-done | bytes 24608 | tf_op jit(solution)/shard_map/ppermute | solution.py:195
  9.7 1.9 %shard_map.95 = (bf16[6,1024,256]{2,1,0:T(8,128)(2,1)S(1)}, bf16[8,128,512]{2,1,0:T(8,128)(2,1)S(1)}, bf16[2,128,512]{2,1,0:T(8,128)(2,1)S(1)}, bf16[2,128,512]{...) custom-call(f32[24,256]{1,0:T(8,128)S(1)} %get-tuple-element.38.refs_0_, ...), custom_call_target="tpu_custom_call" | custom-call | flops 268435456 | bytes 1048576 | tf_op jit(solution)/shard_map/pallas_call | solution.py:203
  11.6 1.1 %collective-permute-start.6 = (bf16[2,128,512]{2,1,0:T(8,128)(2,1)S(1)}, bf16[2,128,512]{2,1,0:T(8,128)(2,1)S(1)}, u32[]{:S(2)}, u32[]{:S(2)}) collective-permute-start(bf16[2,128,512]{2,1,0:T(8,128)(2,1)S(1)} %get-tuple-element.56), channel_id=1, source_target_pairs={{0,224},{16,240},{32,0},{48,16},{64,32},{80,48},{96,64},{112,80},{... | collective-permute-start | bytes 786440 | tf_op jit(solution)/shard_map/ppermute | solution.py:195
  12.6 1.0 %collective-permute-start.7 = (bf16[2,128,512]{2,1,0:T(8,128)(2,1)S(1)}, bf16[2,128,512]{2,1,0:T(8,128)(2,1)S(1)}, u32[]{:S(2)}, u32[]{:S(2)}) collective-permute-start(bf16[2,128,512]{2,1,0:T(8,128)(2,1)S(1)} %get-tuple-element.57), channel_id=1, source_target_pairs={{0,32},{16,48},{32,64},{48,80},{64,96},{80,112},{96,128},{112,144}... | collective-permute-start | bytes 786440 | tf_op jit(solution)/shard_map/ppermute | solution.py:195
  13.7 0.7 %shard_map.96 = (bf16[64,768]{1,0:T(8,128)(2,1)S(1)}, bf16[64,768]{1,0:T(8,128)(2,1)S(1)}, bf16[64,768]{1,0:T(8,128)(2,1)S(1)}, bf16[64,768]{1,0:T(8,128)(2,1)S(1)}) custom-call(bf16[6,1024,256]{2,1,0:T(8,128)(2,1)S(1)} %get-tuple-element.44.ds_ref, bf16[256,1024]{1,0:T(8,128)(2,1)S(1)} %get-tuple-element.45.kt_ref), custom_call_target="tpu_custom_call" | custom-call | flops 268435456 | bytes 1048576 | tf_op jit(solution)/shard_map/pallas_call | solution.py:203
  14.5 0.9 %collective-permute-start.4 = (bf16[64,768]{1,0:T(8,128)(2,1)S(1)}, bf16[64,768]{1,0:T(8,128)(2,1)S(1)}, u32[]{:S(2)}, u32[]{:S(2)}) collective-permute-start(bf16[64,768]{1,0:T(8,128)(2,1)S(1)} %get-tuple-element.48), channel_id=1, source_target_pairs={{0,2},{1,3},{2,0},{3,1},{4,6},{5,7},{6,4},{7,5},{8,10},{9,11},{10,... | collective-permute-start | bytes 294920 | tf_op jit(solution)/shard_map/ppermute | solution.py:195
  15.3 1.0 %collective-permute-start.5 = (bf16[64,768]{1,0:T(8,128)(2,1)S(1)}, bf16[64,768]{1,0:T(8,128)(2,1)S(1)}, u32[]{:S(2)}, u32[]{:S(2)}) collective-permute-start(bf16[64,768]{1,0:T(8,128)(2,1)S(1)} %get-tuple-element.49), channel_id=1, source_target_pairs={{0,3},{1,2},{2,1},{3,0},{4,7},{5,6},{6,5},{7,4},{8,11},{9,10},{10,... | collective-permute-start | bytes 294920 | tf_op jit(solution)/shard_map/ppermute | solution.py:195
  16.3 6.6 %collective-permute-start.8 = (bf16[128,256]{1,0:T(8,128)(2,1)S(1)}, bf16[128,256]{1,0:T(8,128)(2,1)S(1)}, u32[]{:S(2)}, u32[]{:S(2)}) collective-permute-start(bf16[128,256]{1,0:T(8,128)(2,1)S(1)} %get-tuple-element.58), channel_id=1, source_target_pairs={{0,192},{16,208},{32,224},{48,240},{64,0},{80,16},{96,32},{112,48}... | collective-permute-start | bytes 196616 | tf_op jit(solution)/shard_map/ppermute | solution.py:195
  22.9 1.8 %collective-permute-start.9 = (bf16[128,256]{1,0:T(8,128)(2,1)S(1)}, bf16[128,256]{1,0:T(8,128)(2,1)S(1)}, u32[]{:S(2)}, u32[]{:S(2)}) collective-permute-start(bf16[128,256]{1,0:T(8,128)(2,1)S(1)} %get-tuple-element.59), channel_id=1, source_target_pairs={{0,64},{16,80},{32,96},{48,112},{64,128},{80,144},{96,160},{112,17... | collective-permute-start | bytes 196616 | tf_op jit(solution)/shard_map/ppermute | solution.py:195
  24.7 1.5 %shard_map.97 = (bf16[16,3072]{1,0:T(8,128)(2,1)S(1)}, bf16[16,3072]{1,0:T(8,128)(2,1)S(1)}, bf16[16,3072]{1,0:T(8,128)(2,1)S(1)}, bf16[16,3072]{1,0:T(8,128)(2,1)S(1)}) custom-call(bf16[64,768]{1,0:T(8,128)(2,1)S(1)} %get-tuple-element.46.a_ref, bf16[64,768]{1,0:T(8,128)(2,1)S(1)} %collective-permute-done.3.b_ref, ...), custom_call_target="tpu_custom_call" | custom-call | flops 268435456 | bytes 1048576 | tf_op jit(solution)/shard_map/pallas_call | solution.py:203
  26.3 1.7 %collective-permute-start.15 = (bf16[16,3072]{1,0:T(8,128)(2,1)S(1)}, bf16[16,3072]{1,0:T(8,128)(2,1)S(1)}, u32[]{:S(2)}, u32[]{:S(2)}) collective-permute-start(bf16[16,3072]{1,0:T(8,128)(2,1)S(1)} %get-tuple-element.67), channel_id=1, source_target_pairs={{0,4},{4,8},{8,12},{12,0},{1,5},{5,9},{9,13},{13,1},{2,6},{6,10},{... | collective-permute-start | bytes 294920 | tf_op jit(solution)/shard_map/ppermute | solution.py:195
  27.9 2.9 %collective-permute-start.16 = (bf16[16,3072]{1,0:T(8,128)(2,1)S(1)}, bf16[16,3072]{1,0:T(8,128)(2,1)S(1)}, u32[]{:S(2)}, u32[]{:S(2)}) collective-permute-start(bf16[16,3072]{1,0:T(8,128)(2,1)S(1)} %get-tuple-element.68), channel_id=1, source_target_pairs={{0,8},{4,12},{8,0},{12,4},{1,9},{5,13},{9,1},{13,5},{2,10},{6,14},... | collective-permute-start | bytes 294920 | tf_op jit(solution)/shard_map/ppermute | solution.py:195
  30.8 1.6 %collective-permute-start.17 = (bf16[16,3072]{1,0:T(8,128)(2,1)S(1)}, bf16[16,3072]{1,0:T(8,128)(2,1)S(1)}, u32[]{:S(2)}, u32[]{:S(2)}) collective-permute-start(bf16[16,3072]{1,0:T(8,128)(2,1)S(1)} %get-tuple-element.69), channel_id=1, source_target_pairs={{0,12},{4,0},{8,4},{12,8},{1,13},{5,1},{9,5},{13,9},{2,14},{6,2},{... | collective-permute-start | bytes 294920 | tf_op jit(solution)/shard_map/ppermute | solution.py:195
  32.4 0.2 shard_map.98
  32.7 3.0 %collective-permute-start.10 = (bf16[64,512]{1,0:T(8,128)(2,1)S(1)}, bf16[64,512]{1,0:T(8,128)(2,1)S(1)}, u32[]{:S(2)}, u32[]{:S(2)}) collective-permute-start(bf16[64,512]{1,0:T(8,128)(2,1)S(1)} %get-tuple-element.61), channel_id=1, source_target_pairs={{0,192},{16,208},{32,224},{48,240},{64,0},{80,16},{96,32},{112,48}... | collective-permute-start | bytes 196616 | tf_op jit(solution)/shard_map/ppermute | solution.py:195
  35.7 6.3 %collective-permute-start.12 = (bf16[64,512]{1,0:T(8,128)(2,1)S(1)}, bf16[64,512]{1,0:T(8,128)(2,1)S(1)}, u32[]{:S(2)}, u32[]{:S(2)}) collective-permute-start(bf16[64,512]{1,0:T(8,128)(2,1)S(1)} %get-tuple-element.63), channel_id=1, source_target_pairs={{0,208},{16,192},{32,240},{48,224},{64,16},{80,0},{96,48},{112,32}... | collective-permute-start | bytes 196616 | tf_op jit(solution)/shard_map/ppermute | solution.py:195
  42.0 1.8 %collective-permute-start.14 = (bf16[64,512]{1,0:T(8,128)(2,1)S(1)}, bf16[64,512]{1,0:T(8,128)(2,1)S(1)}, u32[]{:S(2)}, u32[]{:S(2)}) collective-permute-start(bf16[64,512]{1,0:T(8,128)(2,1)S(1)} %get-tuple-element.65), channel_id=1, source_target_pairs={{0,16},{16,0},{32,48},{48,32},{64,80},{80,64},{96,112},{112,96},{1... | collective-permute-start | bytes 196616 | tf_op jit(solution)/shard_map/ppermute | solution.py:195
  43.9 7.4 %collective-permute-done.13.refs_3_ = bf16[64,512]{1,0:T(8,128)(2,1)S(1)} collective-permute-done((bf16[64,512]{1,0:T(8,128)(2,1)S(1)}, bf16[64,512]{1,0:T(8,128)(2,1)S(1)}, u32[]{:S(2)}, u32[]{:S(2)}) %collective-permute-start.13) | collective-permute-done | bytes 65568 | tf_op jit(solution)/shard_map/ppermute | solution.py:195
  51.3 0.7 %shard_map.99 = (f32[64,256]{1,0:T(8,128)}, f32[64,256]{1,0:T(8,128)}, bf16[16,3072]{1,0:T(8,128)(2,1)}) custom-call(f32[64,512]{1,0:T(8,128)S(1)} %get-tuple-element.60.keep_ref, bf16[64,512]{1,0:T(8,128)(2,1)S(1)} %collective-permute-done.10.refs_0_, bf16[64,512]{1,0:T(8,128)(2,1)S(1)} %collective-permute-done.11.refs_1_, ...), custom_call_target="tpu_custom_call" | custom-call | flops 268435456 | bytes 1048576 | tf_op jit(solution)/shard_map/pallas_call | solution.py:203
  (18 shorter events, 0.3 us)
Async XLA Ops:
  4.8 3.6 %collective-permute-start.2 = (f32[24,256]{1,0:T(8,128)S(1)}, f32[24,256]{1,0:T(8,128)S(1)}, u32[]{:S(2)}, u32[]{:S(2)}) collective-permute-start(f32[24,256]{1,0:T(8,128)S(1)} %get-tuple-element.38.refs_0_), channel_id=1, source_target_pairs={{0,3},{1,2},{2,1},{3,0},{4,7},{5,6},{6,5},{7,4},{8,11},{9,10},{10,... | collective-permute-start | bytes 73736 | tf_op jit(solution)/shard_map/ppermute | solution.py:195
  5.8 3.8 %collective-permute-start.1 = (f32[24,256]{1,0:T(8,128)S(1)}, f32[24,256]{1,0:T(8,128)S(1)}, u32[]{:S(2)}, u32[]{:S(2)}) collective-permute-start(f32[24,256]{1,0:T(8,128)S(1)} %get-tuple-element.38.refs_0_), channel_id=1, source_target_pairs={{0,2},{1,3},{2,0},{3,1},{4,6},{5,7},{6,4},{7,5},{8,10},{9,11},{10,... | collective-permute-start | bytes 73736 | tf_op jit(solution)/shard_map/ppermute | solution.py:195
  6.5 3.2 %collective-permute-start = (f32[24,256]{1,0:T(8,128)S(1)}, f32[24,256]{1,0:T(8,128)S(1)}, u32[]{:S(2)}, u32[]{:S(2)}) collective-permute-start(f32[24,256]{1,0:T(8,128)S(1)} %get-tuple-element.38.refs_0_), channel_id=1, source_target_pairs={{0,1},{1,0},{2,3},{3,2},{4,5},{5,4},{6,7},{7,6},{8,9},{9,8},{10,11... | collective-permute-start | bytes 73736 | tf_op jit(solution)/shard_map/ppermute | solution.py:195
  11.6 20.9 %collective-permute-start.6 = (bf16[2,128,512]{2,1,0:T(8,128)(2,1)S(1)}, bf16[2,128,512]{2,1,0:T(8,128)(2,1)S(1)}, u32[]{:S(2)}, u32[]{:S(2)}) collective-permute-start(bf16[2,128,512]{2,1,0:T(8,128)(2,1)S(1)} %get-tuple-element.56), channel_id=1, source_target_pairs={{0,224},{16,240},{32,0},{48,16},{64,32},{80,48},{96,64},{112,80},{... | collective-permute-start | bytes 786440 | tf_op jit(solution)/shard_map/ppermute | solution.py:195
  12.6 19.8 %collective-permute-start.7 = (bf16[2,128,512]{2,1,0:T(8,128)(2,1)S(1)}, bf16[2,128,512]{2,1,0:T(8,128)(2,1)S(1)}, u32[]{:S(2)}, u32[]{:S(2)}) collective-permute-start(bf16[2,128,512]{2,1,0:T(8,128)(2,1)S(1)} %get-tuple-element.57), channel_id=1, source_target_pairs={{0,32},{16,48},{32,64},{48,80},{64,96},{80,112},{96,128},{112,144}... | collective-permute-start | bytes 786440 | tf_op jit(solution)/shard_map/ppermute | solution.py:195
  14.4 2.0 %collective-permute-start.3 = (bf16[64,768]{1,0:T(8,128)(2,1)S(1)}, bf16[64,768]{1,0:T(8,128)(2,1)S(1)}, u32[]{:S(2)}, u32[]{:S(2)}) collective-permute-start(bf16[64,768]{1,0:T(8,128)(2,1)S(1)} %get-tuple-element.47), channel_id=1, source_target_pairs={{0,1},{1,0},{2,3},{3,2},{4,5},{5,4},{6,7},{7,6},{8,9},{9,8},{10,11... | collective-permute-start | bytes 294920 | tf_op jit(solution)/shard_map/ppermute | solution.py:195
  14.5 8.5 %collective-permute-start.4 = (bf16[64,768]{1,0:T(8,128)(2,1)S(1)}, bf16[64,768]{1,0:T(8,128)(2,1)S(1)}, u32[]{:S(2)}, u32[]{:S(2)}) collective-permute-start(bf16[64,768]{1,0:T(8,128)(2,1)S(1)} %get-tuple-element.48), channel_id=1, source_target_pairs={{0,2},{1,3},{2,0},{3,1},{4,6},{5,7},{6,4},{7,5},{8,10},{9,11},{10,... | collective-permute-start | bytes 294920 | tf_op jit(solution)/shard_map/ppermute | solution.py:195
  15.3 9.4 %collective-permute-start.5 = (bf16[64,768]{1,0:T(8,128)(2,1)S(1)}, bf16[64,768]{1,0:T(8,128)(2,1)S(1)}, u32[]{:S(2)}, u32[]{:S(2)}) collective-permute-start(bf16[64,768]{1,0:T(8,128)(2,1)S(1)} %get-tuple-element.49), channel_id=1, source_target_pairs={{0,3},{1,2},{2,1},{3,0},{4,7},{5,6},{6,5},{7,4},{8,11},{9,10},{10,... | collective-permute-start | bytes 294920 | tf_op jit(solution)/shard_map/ppermute | solution.py:195
  16.3 11.6 %collective-permute-start.8 = (bf16[128,256]{1,0:T(8,128)(2,1)S(1)}, bf16[128,256]{1,0:T(8,128)(2,1)S(1)}, u32[]{:S(2)}, u32[]{:S(2)}) collective-permute-start(bf16[128,256]{1,0:T(8,128)(2,1)S(1)} %get-tuple-element.58), channel_id=1, source_target_pairs={{0,192},{16,208},{32,224},{48,240},{64,0},{80,16},{96,32},{112,48}... | collective-permute-start | bytes 196616 | tf_op jit(solution)/shard_map/ppermute | solution.py:195
  22.9 7.9 %collective-permute-start.9 = (bf16[128,256]{1,0:T(8,128)(2,1)S(1)}, bf16[128,256]{1,0:T(8,128)(2,1)S(1)}, u32[]{:S(2)}, u32[]{:S(2)}) collective-permute-start(bf16[128,256]{1,0:T(8,128)(2,1)S(1)} %get-tuple-element.59), channel_id=1, source_target_pairs={{0,64},{16,80},{32,96},{48,112},{64,128},{80,144},{96,160},{112,17... | collective-permute-start | bytes 196616 | tf_op jit(solution)/shard_map/ppermute | solution.py:195
  26.3 9.4 %collective-permute-start.15 = (bf16[16,3072]{1,0:T(8,128)(2,1)S(1)}, bf16[16,3072]{1,0:T(8,128)(2,1)S(1)}, u32[]{:S(2)}, u32[]{:S(2)}) collective-permute-start(bf16[16,3072]{1,0:T(8,128)(2,1)S(1)} %get-tuple-element.67), channel_id=1, source_target_pairs={{0,4},{4,8},{8,12},{12,0},{1,5},{5,9},{9,13},{13,1},{2,6},{6,10},{... | collective-permute-start | bytes 294920 | tf_op jit(solution)/shard_map/ppermute | solution.py:195
  27.9 14.0 %collective-permute-start.16 = (bf16[16,3072]{1,0:T(8,128)(2,1)S(1)}, bf16[16,3072]{1,0:T(8,128)(2,1)S(1)}, u32[]{:S(2)}, u32[]{:S(2)}) collective-permute-start(bf16[16,3072]{1,0:T(8,128)(2,1)S(1)} %get-tuple-element.68), channel_id=1, source_target_pairs={{0,8},{4,12},{8,0},{12,4},{1,9},{5,13},{9,1},{13,5},{2,10},{6,14},... | collective-permute-start | bytes 294920 | tf_op jit(solution)/shard_map/ppermute | solution.py:195
  30.8 11.1 %collective-permute-start.17 = (bf16[16,3072]{1,0:T(8,128)(2,1)S(1)}, bf16[16,3072]{1,0:T(8,128)(2,1)S(1)}, u32[]{:S(2)}, u32[]{:S(2)}) collective-permute-start(bf16[16,3072]{1,0:T(8,128)(2,1)S(1)} %get-tuple-element.69), channel_id=1, source_target_pairs={{0,12},{4,0},{8,4},{12,8},{1,13},{5,1},{9,5},{13,9},{2,14},{6,2},{... | collective-permute-start | bytes 294920 | tf_op jit(solution)/shard_map/ppermute | solution.py:195
  32.7 11.1 %collective-permute-start.10 = (bf16[64,512]{1,0:T(8,128)(2,1)S(1)}, bf16[64,512]{1,0:T(8,128)(2,1)S(1)}, u32[]{:S(2)}, u32[]{:S(2)}) collective-permute-start(bf16[64,512]{1,0:T(8,128)(2,1)S(1)} %get-tuple-element.61), channel_id=1, source_target_pairs={{0,192},{16,208},{32,224},{48,240},{64,0},{80,16},{96,32},{112,48}... | collective-permute-start | bytes 196616 | tf_op jit(solution)/shard_map/ppermute | solution.py:195
  35.6 8.1 %collective-permute-start.11 = (bf16[64,512]{1,0:T(8,128)(2,1)S(1)}, bf16[64,512]{1,0:T(8,128)(2,1)S(1)}, u32[]{:S(2)}, u32[]{:S(2)}) collective-permute-start(bf16[64,512]{1,0:T(8,128)(2,1)S(1)} %get-tuple-element.62), channel_id=1, source_target_pairs={{0,64},{16,80},{32,96},{48,112},{64,128},{80,144},{96,160},{112,17... | collective-permute-start | bytes 196616 | tf_op jit(solution)/shard_map/ppermute | solution.py:195
  35.7 8.2 %collective-permute-start.12 = (bf16[64,512]{1,0:T(8,128)(2,1)S(1)}, bf16[64,512]{1,0:T(8,128)(2,1)S(1)}, u32[]{:S(2)}, u32[]{:S(2)}) collective-permute-start(bf16[64,512]{1,0:T(8,128)(2,1)S(1)} %get-tuple-element.63), channel_id=1, source_target_pairs={{0,208},{16,192},{32,240},{48,224},{64,16},{80,0},{96,48},{112,32}... | collective-permute-start | bytes 196616 | tf_op jit(solution)/shard_map/ppermute | solution.py:195
  42.0 9.3 %collective-permute-start.13 = (bf16[64,512]{1,0:T(8,128)(2,1)S(1)}, bf16[64,512]{1,0:T(8,128)(2,1)S(1)}, u32[]{:S(2)}, u32[]{:S(2)}) collective-permute-start(bf16[64,512]{1,0:T(8,128)(2,1)S(1)} %get-tuple-element.64), channel_id=1, source_target_pairs={{0,80},{16,64},{32,112},{48,96},{64,144},{80,128},{96,176},{112,16... | collective-permute-start | bytes 196616 | tf_op jit(solution)/shard_map/ppermute | solution.py:195
  42.0 9.3 %collective-permute-start.14 = (bf16[64,512]{1,0:T(8,128)(2,1)S(1)}, bf16[64,512]{1,0:T(8,128)(2,1)S(1)}, u32[]{:S(2)}, u32[]{:S(2)}) collective-permute-start(bf16[64,512]{1,0:T(8,128)(2,1)S(1)} %get-tuple-element.65), channel_id=1, source_target_pairs={{0,16},{16,0},{32,48},{48,32},{64,80},{80,64},{96,112},{112,96},{1... | collective-permute-start | bytes 196616 | tf_op jit(solution)/shard_map/ppermute | solution.py:195

commit v3 on v2

--- a/solution.py
+++ b/solution.py
@@ -134,25 +134,24 @@
     return sum(t.astype(F32) for t in terms)
 
 
-def collect_kernel(kv_ref, above_ref, below_ref, far_k, far_v,
-                   down_same, down_other, up_same, up_other, keep_ref, mine_other, both):
-    rows, w = keep_ref.shape[0], far_k.shape[1]
+def collect_kernel(kv_ref, above_ref, below_ref, far_k, far_v, to_down, to_up, mine_ref):
+    w = far_k.shape[1]
+    down, up = kv_ref.at[away(-2)], kv_ref.at[away(2)]
+    to_down[:, :w] = total_of(down[:, :w], above_ref[1, :, :w], far_k[...]).astype(BF16)
+    to_down[:, w:] = total_of(down[:, w:], above_ref[1, :, w:]).astype(BF16)
+    to_up[:, :w] = total_of(up[:, :w], below_ref[1, :, :w]).astype(BF16)
+    to_up[:, w:] = total_of(up[:, w:], below_ref[1, :, w:], far_v[...]).astype(BF16)
+    mine_ref[...] = total_of(kv_ref[away(0)], above_ref[0], below_ref[0])
+
+
+def last_join_kernel(mine_ref, down_ref, up_ref, keep_ref, send_ref, both):
+    rows = keep_ref.shape[0]
+    mine = total_of(mine_ref[...], down_ref[...], up_ref[...])
+    both[0] = mine[:rows]
+    both[1] = mine[rows:]
     part = lax.rem(lax.axis_index("section"), 2)
-    mine = total_of(kv_ref[away(0)], above_ref[0], below_ref[0])
-    for xh in range(2):
-        both[xh] = mine[xh * rows:(xh + 1) * rows, :]
     keep_ref[...] = both[part]
-    mine_other[...] = both[1 - part].astype(BF16)
-    for by, near, far, cols, same, other in (
-        (-2, above_ref, far_k, slice(0, w), down_same, down_other),
-        (2, below_ref, far_v, slice(w, 2 * w), up_same, up_other),
-    ):
-        whole = total_of(kv_ref[away(by)], near[1])
-        for xh in range(2):
-            both[xh] = whole[xh * rows:(xh + 1) * rows, :]
-            both[xh, :, cols] += far[xh * rows:(xh + 1) * rows, :].astype(F32)
-        same[...] = both[part].astype(BF16)
-        other[...] = both[1 - part].astype(BF16)
+    send_ref[...] = both[1 - part].astype(BF16)
 
 
 def query_grad_kernel(ds_ref, kt_ref, o0, o1, o2, o3, all_ref):
@@ -183,8 +182,8 @@
 
 
 def finish_kernel(keep_ref, *refs):
-    got, parts, (key_ref, value_ref, input_ref) = refs[:5], refs[5:9], refs[9:]
-    total = total_of(keep_ref[...], *(r[...] for r in got))
+    got, parts, (key_ref, value_ref, input_ref) = refs[0], refs[1:5], refs[5:]
+    total = total_of(keep_ref[...], got[...])
     width = key_ref.shape[1]
     key_ref[...] = total[:, :width]
     value_ref[...] = total[:, width:]
@@ -248,33 +247,32 @@
         [on((rows, heads * HD), BF16)] * 4, (ds, kt),
         scratch=[on((4, rows, heads * HD), BF16)],
     )
+    kv, parts = lax.optimization_barrier((kv, parts))
     parts = [parts[0]] + [moved(parts[by], "key", lambda i: i ^ by) for by in (1, 2, 3)]
+    whole = on((slab, 2 * width), BF16)
+    down, up, mine = call(
+        collect_kernel, [whole, whole, on((slab, 2 * width), F32)], (kv, above, below, far_k, far_v)
+    )
+    mine, parts = lax.optimization_barrier((mine, parts))
+    down = moved(down, "section", deeper(-2))
+    up = moved(up, "section", deeper(2))
     parts = call(
         project_kernel,
         [on((rows // 4, d_model), BF16)] * 4, (*parts, w),
         scratch=[on((4, rows // 4, d_model), BF16)],
     )
-    kv, parts = lax.optimization_barrier((kv, parts))
-    piece = on((slab // 2, 2 * width), BF16)
-    down_same, down_other, up_same, up_other, keep, mine_other = call(
-        collect_kernel,
-        [piece] * 4 + [on((slab // 2, 2 * width), F32), piece],
-        (kv, above, below, far_k, far_v),
+    parts = [parts[0]] + [moved(parts[by], "head", lambda i: (i + by) % 4) for by in (1, 2, 3)]
+    keep, send = call(
+        last_join_kernel,
+        [on((slab // 2, 2 * width), F32), on((slab // 2, 2 * width), BF16)], (mine, down, up),
         scratch=[on((2, slab // 2, 2 * width), F32)],
     )
-    got = [
-        moved(down_same, "section", deeper(-2)),
-        moved(up_same, "section", deeper(2)),
-        moved(down_other, "section", deeper(-2, 1)),
-        moved(up_other, "section", deeper(2, 1)),
-        moved(mine_other, "section", deeper(0, 1)),
-    ]
-    parts = [parts[0]] + [moved(parts[by], "head", lambda i: (i + by) % 4) for by in (1, 2, 3)]
+    got = moved(send, "section", deeper(0, 1))
     key_grad, value_grad, input_grad = call(
         finish_kernel,
         [jax.ShapeDtypeStruct((slab // 2, width), F32), jax.ShapeDtypeStruct((slab // 2, width), F32),
          jax.ShapeDtypeStruct((rows // 4, d_model), BF16)],
-        (keep, *got, *parts),
+        (keep, got, *parts),
     )
     return input_grad[None], key_grad, value_grad
 

time: 52.2 us -> 49.3 us (0.944)
  the two profiles are of different devices: /device:TPU:32 before, /device:TPU:8 now
where the time goes in v3:
time: 49.3 us; the launch traced here: 49.2 us
  starting transfers between devices  23.1 us (47%)
  waiting for transfers between devices  16.2 us (33%)
  Pallas kernels  9.22 us (19%)
  between operations  0.69 us (1%)
    ppermute x16, starting transfers between devices, moved(): lax.ppermute(x, axis, [(i, to(i)) for i in range(lax.axis_size(axis))])  23.1 us
    ppermute x16, waiting for transfers between devices, moved(): lax.ppermute(x, axis, [(i, to(i)) for i in range(lax.axis_size(axis))])  16.2 us
    pallas_call x7, Pallas kernels, call(): pl.pallas_call(kernel, in_specs=specs or [VMEM] * len(ins), out_specs=[VM...  9.22 us
  transfers between devices with their start and end apart: 16, of which 8 were waited for; matrix products, arithmetic and copies ran while one was open for 0% of the time, Pallas kernels for 5%

profile of v3, /device:TPU:8, one launch (start us, length us, event | category | flops | bytes accessed | tf_op | source)
XLA Modules:
  0.0 49.2 jit_solution(15823289826397875830)
XLA Ops:
  0.6 4.2 %shard_map.94 = (f32[6,1024,256]{2,1,0:T(8,128)S(1)}, f32[6,1024,256]{2,1,0:T(8,128)S(1)}, bf16[256,1024]{1,0:T(8,128)(2,1)S(1)}, f32[24,256]{1,0:T(8,128)S(1)},...) custom-call(s32[2,16]{1,0:T(2,128)} %bitcast.9, s32[2,16]{1,0:T(2,128)} %bitcast.10, ...), custom_call_target="tpu_custom_call" | custom-call | flops 268435456 | bytes 1048576 | tf_op jit(solution)/shard_map/pallas_call | solution.py:202
  4.8 1.0 %collective-permute-start.2 = (f32[24,256]{1,0:T(8,128)S(1)}, f32[24,256]{1,0:T(8,128)S(1)}, u32[]{:S(2)}, u32[]{:S(2)}) collective-permute-start(f32[24,256]{1,0:T(8,128)S(1)} %get-tuple-element.42.refs_0_), channel_id=1, source_target_pairs={{0,3},{1,2},{2,1},{3,0},{4,7},{5,6},{6,5},{7,4},{8,11},{9,10},{10,... | collective-permute-start | bytes 73736 | tf_op jit(solution)/shard_map/ppermute | solution.py:194
  5.8 0.7 %collective-permute-start.1 = (f32[24,256]{1,0:T(8,128)S(1)}, f32[24,256]{1,0:T(8,128)S(1)}, u32[]{:S(2)}, u32[]{:S(2)}) collective-permute-start(f32[24,256]{1,0:T(8,128)S(1)} %get-tuple-element.42.refs_0_), channel_id=1, source_target_pairs={{0,2},{1,3},{2,0},{3,1},{4,6},{5,7},{6,4},{7,5},{8,10},{9,11},{10,... | collective-permute-start | bytes 73736 | tf_op jit(solution)/shard_map/ppermute | solution.py:194
  6.8 1.6 %collective-permute-done.2.refs_3_ = f32[24,256]{1,0:T(8,128)S(1)} collective-permute-done((f32[24,256]{1,0:T(8,128)S(1)}, f32[24,256]{1,0:T(8,128)S(1)}, u32[]{:S(2)}, u32[]{:S(2)}) %collective-permute-start.2) | collective-permute-done | bytes 24608 | tf_op jit(solution)/shard_map/ppermute | solution.py:194
  8.4 1.3 %collective-permute-done.1.refs_2_ = f32[24,256]{1,0:T(8,128)S(1)} collective-permute-done((f32[24,256]{1,0:T(8,128)S(1)}, f32[24,256]{1,0:T(8,128)S(1)}, u32[]{:S(2)}, u32[]{:S(2)}) %collective-permute-start.1) | collective-permute-done | bytes 24608 | tf_op jit(solution)/shard_map/ppermute | solution.py:194
  9.7 1.9 %shard_map.95 = (bf16[6,1024,256]{2,1,0:T(8,128)(2,1)S(1)}, bf16[8,128,512]{2,1,0:T(8,128)(2,1)S(1)}, bf16[2,128,512]{2,1,0:T(8,128)(2,1)S(1)}, bf16[2,128,512]{...) custom-call(f32[24,256]{1,0:T(8,128)S(1)} %get-tuple-element.42.refs_0_, ...), custom_call_target="tpu_custom_call" | custom-call | flops 268435456 | bytes 1048576 | tf_op jit(solution)/shard_map/pallas_call | solution.py:202
  11.6 5.9 %collective-permute-start.3 = (bf16[2,128,512]{2,1,0:T(8,128)(2,1)S(1)}, bf16[2,128,512]{2,1,0:T(8,128)(2,1)S(1)}, u32[]{:S(2)}, u32[]{:S(2)}) collective-permute-start(bf16[2,128,512]{2,1,0:T(8,128)(2,1)S(1)} %get-tuple-element.55), channel_id=1, source_target_pairs={{0,224},{16,240},{32,0},{48,16},{64,32},{80,48},{96,64},{112,80},{... | collective-permute-start | bytes 786440 | tf_op jit(solution)/shard_map/ppermute | solution.py:194
  17.5 2.5 %collective-permute-start.5 = (bf16[128,256]{1,0:T(8,128)(2,1)S(1)}, bf16[128,256]{1,0:T(8,128)(2,1)S(1)}, u32[]{:S(2)}, u32[]{:S(2)}) collective-permute-start(bf16[128,256]{1,0:T(8,128)(2,1)S(1)} %get-tuple-element.57), channel_id=1, source_target_pairs={{0,192},{16,208},{32,224},{48,240},{64,0},{80,16},{96,32},{112,48}... | collective-permute-start | bytes 196616 | tf_op jit(solution)/shard_map/ppermute | solution.py:194
  20.0 0.5 collective-permute-start.6
  20.4 0.7 %shard_map.96 = (bf16[64,768]{1,0:T(8,128)(2,1)S(1)}, bf16[64,768]{1,0:T(8,128)(2,1)S(1)}, bf16[64,768]{1,0:T(8,128)(2,1)S(1)}, bf16[64,768]{1,0:T(8,128)(2,1)S(1)}) custom-call(bf16[6,1024,256]{2,1,0:T(8,128)(2,1)S(1)} %get-tuple-element.48.ds_ref, bf16[256,1024]{1,0:T(8,128)(2,1)S(1)} %get-tuple-element.49.kt_ref), custom_call_target="tpu_custom_call" | custom-call | flops 268435456 | bytes 1048576 | tf_op jit(solution)/shard_map/pallas_call | solution.py:202
  21.2 4.3 %collective-permute-done.5.far_k = bf16[128,256]{1,0:T(8,128)(2,1)S(1)} collective-permute-done((bf16[128,256]{1,0:T(8,128)(2,1)S(1)}, bf16[128,256]{1,0:T(8,128)(2,1)S(1)}, u32[]{:S(2)}, u32[]{:S(2)}) %collective-permute-start.5) | collective-permute-done | bytes 65568 | tf_op jit(solution)/shard_map/ppermute | solution.py:194
  25.6 1.2 %collective-permute-start.8 = (bf16[64,768]{1,0:T(8,128)(2,1)S(1)}, bf16[64,768]{1,0:T(8,128)(2,1)S(1)}, u32[]{:S(2)}, u32[]{:S(2)}) collective-permute-start(bf16[64,768]{1,0:T(8,128)(2,1)S(1)} %get-tuple-element.62), channel_id=1, source_target_pairs={{0,2},{1,3},{2,0},{3,1},{4,6},{5,7},{6,4},{7,5},{8,10},{9,11},{10,... | collective-permute-start | bytes 294920 | tf_op jit(solution)/shard_map/ppermute | solution.py:194
  26.8 0.9 %collective-permute-done.6.far_v = bf16[128,256]{1,0:T(8,128)(2,1)S(1)} collective-permute-done((bf16[128,256]{1,0:T(8,128)(2,1)S(1)}, bf16[128,256]{1,0:T(8,128)(2,1)S(1)}, u32[]{:S(2)}, u32[]{:S(2)}) %collective-permute-start.6) | collective-permute-done | bytes 65568 | tf_op jit(solution)/shard_map/ppermute | solution.py:194
  27.6 0.6 %collective-permute-done.4.below_ref = bf16[2,128,512]{2,1,0:T(8,128)(2,1)S(1)} collective-permute-done((bf16[2,128,512]{2,1,0:T(8,128)(2,1)S(1)}, bf16[2,128,512]{2,1,0:T(8,128)(2,1)S(1)}, u32[]{:S(2)}, u32[]{:S(2)}) %collective-permute-start.4) | collective-permute-done | bytes 262176 | tf_op jit(solution)/shard_map/ppermute | solution.py:194
  28.4 3.4 %collective-permute-start.10 = (bf16[128,512]{1,0:T(8,128)(2,1)S(1)}, bf16[128,512]{1,0:T(8,128)(2,1)S(1)}, u32[]{:S(2)}, u32[]{:S(2)}) collective-permute-start(bf16[128,512]{1,0:T(8,128)(2,1)S(1)} %get-tuple-element.65), channel_id=1, source_target_pairs={{0,192},{16,208},{32,224},{48,240},{64,0},{80,16},{96,32},{112,48}... | collective-permute-start | bytes 393224 | tf_op jit(solution)/shard_map/ppermute | solution.py:194
  31.8 0.7 %collective-permute-done.9.d_ref = bf16[64,768]{1,0:T(8,128)(2,1)S(1)} collective-permute-done((bf16[64,768]{1,0:T(8,128)(2,1)S(1)}, bf16[64,768]{1,0:T(8,128)(2,1)S(1)}, u32[]{:S(2)}, u32[]{:S(2)}) %collective-permute-start.9) | collective-permute-done | bytes 98336 | tf_op jit(solution)/shard_map/ppermute | solution.py:194
  32.5 1.5 %shard_map.99 = (bf16[16,3072]{1,0:T(8,128)(2,1)S(1)}, bf16[16,3072]{1,0:T(8,128)(2,1)S(1)}, bf16[16,3072]{1,0:T(8,128)(2,1)S(1)}, bf16[16,3072]{1,0:T(8,128)(2,1)S(1)}) custom-call(bf16[64,768]{1,0:T(8,128)(2,1)S(1)} %get-tuple-element.69.a_ref, bf16[64,768]{1,0:T(8,128)(2,1)S(1)} %collective-permute-done.7.b_ref, ...), custom_call_target="tpu_custom_call" | custom-call | flops 268435456 | bytes 1048576 | tf_op jit(solution)/shard_map/pallas_call | solution.py:202
  34.0 1.7 %collective-permute-start.13 = (bf16[16,3072]{1,0:T(8,128)(2,1)S(1)}, bf16[16,3072]{1,0:T(8,128)(2,1)S(1)}, u32[]{:S(2)}, u32[]{:S(2)}) collective-permute-start(bf16[16,3072]{1,0:T(8,128)(2,1)S(1)} %get-tuple-element.75), channel_id=1, source_target_pairs={{0,4},{4,8},{8,12},{12,0},{1,5},{5,9},{9,13},{13,1},{2,6},{6,10},{... | collective-permute-start | bytes 294920 | tf_op jit(solution)/shard_map/ppermute | solution.py:194
  35.7 0.9 %collective-permute-start.14 = (bf16[16,3072]{1,0:T(8,128)(2,1)S(1)}, bf16[16,3072]{1,0:T(8,128)(2,1)S(1)}, u32[]{:S(2)}, u32[]{:S(2)}) collective-permute-start(bf16[16,3072]{1,0:T(8,128)(2,1)S(1)} %get-tuple-element.76), channel_id=1, source_target_pairs={{0,8},{4,12},{8,0},{12,4},{1,9},{5,13},{9,1},{13,5},{2,10},{6,14},... | collective-permute-start | bytes 294920 | tf_op jit(solution)/shard_map/ppermute | solution.py:194
  36.6 2.4 %collective-permute-start.15 = (bf16[16,3072]{1,0:T(8,128)(2,1)S(1)}, bf16[16,3072]{1,0:T(8,128)(2,1)S(1)}, u32[]{:S(2)}, u32[]{:S(2)}) collective-permute-start(bf16[16,3072]{1,0:T(8,128)(2,1)S(1)} %get-tuple-element.77), channel_id=1, source_target_pairs={{0,12},{4,0},{8,4},{12,8},{1,13},{5,1},{9,5},{13,9},{2,14},{6,2},{... | collective-permute-start | bytes 294920 | tf_op jit(solution)/shard_map/ppermute | solution.py:194
  39.0 3.5 %collective-permute-done.11.up_ref = bf16[128,512]{1,0:T(8,128)(2,1)S(1)} collective-permute-done((bf16[128,512]{1,0:T(8,128)(2,1)S(1)}, bf16[128,512]{1,0:T(8,128)(2,1)S(1)}, u32[]{:S(2)}, u32[]{:S(2)}) %collective-permute-start.11) | collective-permute-done | bytes 131104 | tf_op jit(solution)/shard_map/ppermute | solution.py:194
  42.6 2.6 %collective-permute-start.12 = (bf16[64,512]{1,0:T(8,128)(2,1)S(1)}, bf16[64,512]{1,0:T(8,128)(2,1)S(1)}, u32[]{:S(2)}, u32[]{:S(2)}) collective-permute-start(bf16[64,512]{1,0:T(8,128)(2,1)S(1)} %get-tuple-element.68), channel_id=1, source_target_pairs={{0,16},{16,0},{32,48},{48,32},{64,80},{80,64},{96,112},{112,96},{1... | collective-permute-start | bytes 196616 | tf_op jit(solution)/shard_map/ppermute | solution.py:194
  45.2 3.3 %collective-permute-done.12.refs_0_ = bf16[64,512]{1,0:T(8,128)(2,1)S(1)} collective-permute-done((bf16[64,512]{1,0:T(8,128)(2,1)S(1)}, bf16[64,512]{1,0:T(8,128)(2,1)S(1)}, u32[]{:S(2)}, u32[]{:S(2)}) %collective-permute-start.12) | collective-permute-done | bytes 65568 | tf_op jit(solution)/shard_map/ppermute | solution.py:194
  48.4 0.7 %shard_map.100 = (f32[64,256]{1,0:T(8,128)}, f32[64,256]{1,0:T(8,128)}, bf16[16,3072]{1,0:T(8,128)(2,1)}) custom-call(f32[64,512]{1,0:T(8,128)S(1)} %get-tuple-element.67.keep_ref, bf16[64,512]{1,0:T(8,128)(2,1)S(1)} %collective-permute-done.12.refs_0_, bf16[16,3072]{1,0:T(8,128)(2,1)S(1)} %get-tuple-element.74.refs_1_, ...), custom_call_target="tpu_custom_call" | custom-call | flops 268435456 | bytes 1048576 | tf_op jit(solution)/shard_map/pallas_call | solution.py:202
  (15 shorter events, 0.6 us)
Async XLA Ops:
  4.8 3.6 %collective-permute-start.2 = (f32[24,256]{1,0:T(8,128)S(1)}, f32[24,256]{1,0:T(8,128)S(1)}, u32[]{:S(2)}, u32[]{:S(2)}) collective-permute-start(f32[24,256]{1,0:T(8,128)S(1)} %get-tuple-element.42.refs_0_), channel_id=1, source_target_pairs={{0,3},{1,2},{2,1},{3,0},{4,7},{5,6},{6,5},{7,4},{8,11},{9,10},{10,... | collective-permute-start | bytes 73736 | tf_op jit(solution)/shard_map/ppermute | solution.py:194
  5.8 3.8 %collective-permute-start.1 = (f32[24,256]{1,0:T(8,128)S(1)}, f32[24,256]{1,0:T(8,128)S(1)}, u32[]{:S(2)}, u32[]{:S(2)}) collective-permute-start(f32[24,256]{1,0:T(8,128)S(1)} %get-tuple-element.42.refs_0_), channel_id=1, source_target_pairs={{0,2},{1,3},{2,0},{3,1},{4,6},{5,7},{6,4},{7,5},{8,10},{9,11},{10,... | collective-permute-start | bytes 73736 | tf_op jit(solution)/shard_map/ppermute | solution.py:194
  6.5 3.2 %collective-permute-start = (f32[24,256]{1,0:T(8,128)S(1)}, f32[24,256]{1,0:T(8,128)S(1)}, u32[]{:S(2)}, u32[]{:S(2)}) collective-permute-start(f32[24,256]{1,0:T(8,128)S(1)} %get-tuple-element.42.refs_0_), channel_id=1, source_target_pairs={{0,1},{1,0},{2,3},{3,2},{4,5},{5,4},{6,7},{7,6},{8,9},{9,8},{10,11... | collective-permute-start | bytes 73736 | tf_op jit(solution)/shard_map/ppermute | solution.py:194
  11.6 16.1 %collective-permute-start.3 = (bf16[2,128,512]{2,1,0:T(8,128)(2,1)S(1)}, bf16[2,128,512]{2,1,0:T(8,128)(2,1)S(1)}, u32[]{:S(2)}, u32[]{:S(2)}) collective-permute-start(bf16[2,128,512]{2,1,0:T(8,128)(2,1)S(1)} %get-tuple-element.55), channel_id=1, source_target_pairs={{0,224},{16,240},{32,0},{48,16},{64,32},{80,48},{96,64},{112,80},{... | collective-permute-start | bytes 786440 | tf_op jit(solution)/shard_map/ppermute | solution.py:194
  17.5 10.8 %collective-permute-start.4 = (bf16[2,128,512]{2,1,0:T(8,128)(2,1)S(1)}, bf16[2,128,512]{2,1,0:T(8,128)(2,1)S(1)}, u32[]{:S(2)}, u32[]{:S(2)}) collective-permute-start(bf16[2,128,512]{2,1,0:T(8,128)(2,1)S(1)} %get-tuple-element.56), channel_id=1, source_target_pairs={{0,32},{16,48},{32,64},{48,80},{64,96},{80,112},{96,128},{112,144}... | collective-permute-start | bytes 786440 | tf_op jit(solution)/shard_map/ppermute | solution.py:194
  17.5 8.1 %collective-permute-start.5 = (bf16[128,256]{1,0:T(8,128)(2,1)S(1)}, bf16[128,256]{1,0:T(8,128)(2,1)S(1)}, u32[]{:S(2)}, u32[]{:S(2)}) collective-permute-start(bf16[128,256]{1,0:T(8,128)(2,1)S(1)} %get-tuple-element.57), channel_id=1, source_target_pairs={{0,192},{16,208},{32,224},{48,240},{64,0},{80,16},{96,32},{112,48}... | collective-permute-start | bytes 196616 | tf_op jit(solution)/shard_map/ppermute | solution.py:194
  20.0 7.7 %collective-permute-start.6 = (bf16[128,256]{1,0:T(8,128)(2,1)S(1)}, bf16[128,256]{1,0:T(8,128)(2,1)S(1)}, u32[]{:S(2)}, u32[]{:S(2)}) collective-permute-start(bf16[128,256]{1,0:T(8,128)(2,1)S(1)} %get-tuple-element.58), channel_id=1, source_target_pairs={{0,64},{16,80},{32,96},{48,112},{64,128},{80,144},{96,160},{112,17... | collective-permute-start | bytes 196616 | tf_op jit(solution)/shard_map/ppermute | solution.py:194
  21.1 10.7 %collective-permute-start.7 = (bf16[64,768]{1,0:T(8,128)(2,1)S(1)}, bf16[64,768]{1,0:T(8,128)(2,1)S(1)}, u32[]{:S(2)}, u32[]{:S(2)}) collective-permute-start(bf16[64,768]{1,0:T(8,128)(2,1)S(1)} %get-tuple-element.61), channel_id=1, source_target_pairs={{0,1},{1,0},{2,3},{3,2},{4,5},{5,4},{6,7},{7,6},{8,9},{9,8},{10,11... | collective-permute-start | bytes 294920 | tf_op jit(solution)/shard_map/ppermute | solution.py:194
  25.6 6.2 %collective-permute-start.8 = (bf16[64,768]{1,0:T(8,128)(2,1)S(1)}, bf16[64,768]{1,0:T(8,128)(2,1)S(1)}, u32[]{:S(2)}, u32[]{:S(2)}) collective-permute-start(bf16[64,768]{1,0:T(8,128)(2,1)S(1)} %get-tuple-element.62), channel_id=1, source_target_pairs={{0,2},{1,3},{2,0},{3,1},{4,6},{5,7},{6,4},{7,5},{8,10},{9,11},{10,... | collective-permute-start | bytes 294920 | tf_op jit(solution)/shard_map/ppermute | solution.py:194
  27.6 4.8 %collective-permute-start.9 = (bf16[64,768]{1,0:T(8,128)(2,1)S(1)}, bf16[64,768]{1,0:T(8,128)(2,1)S(1)}, u32[]{:S(2)}, u32[]{:S(2)}) collective-permute-start(bf16[64,768]{1,0:T(8,128)(2,1)S(1)} %get-tuple-element.63), channel_id=1, source_target_pairs={{0,3},{1,2},{2,1},{3,0},{4,7},{5,6},{6,5},{7,4},{8,11},{9,10},{10,... | collective-permute-start | bytes 294920 | tf_op jit(solution)/shard_map/ppermute | solution.py:194
  28.4 10.6 %collective-permute-start.10 = (bf16[128,512]{1,0:T(8,128)(2,1)S(1)}, bf16[128,512]{1,0:T(8,128)(2,1)S(1)}, u32[]{:S(2)}, u32[]{:S(2)}) collective-permute-start(bf16[128,512]{1,0:T(8,128)(2,1)S(1)} %get-tuple-element.65), channel_id=1, source_target_pairs={{0,192},{16,208},{32,224},{48,240},{64,0},{80,16},{96,32},{112,48}... | collective-permute-start | bytes 393224 | tf_op jit(solution)/shard_map/ppermute | solution.py:194
  31.8 10.7 %collective-permute-start.11 = (bf16[128,512]{1,0:T(8,128)(2,1)S(1)}, bf16[128,512]{1,0:T(8,128)(2,1)S(1)}, u32[]{:S(2)}, u32[]{:S(2)}) collective-permute-start(bf16[128,512]{1,0:T(8,128)(2,1)S(1)} %get-tuple-element.66), channel_id=1, source_target_pairs={{0,64},{16,80},{32,96},{48,112},{64,128},{80,144},{96,160},{112,17... | collective-permute-start | bytes 393224 | tf_op jit(solution)/shard_map/ppermute | solution.py:194
  34.0 11.2 %collective-permute-start.13 = (bf16[16,3072]{1,0:T(8,128)(2,1)S(1)}, bf16[16,3072]{1,0:T(8,128)(2,1)S(1)}, u32[]{:S(2)}, u32[]{:S(2)}) collective-permute-start(bf16[16,3072]{1,0:T(8,128)(2,1)S(1)} %get-tuple-element.75), channel_id=1, source_target_pairs={{0,4},{4,8},{8,12},{12,0},{1,5},{5,9},{9,13},{13,1},{2,6},{6,10},{... | collective-permute-start | bytes 294920 | tf_op jit(solution)/shard_map/ppermute | solution.py:194
  35.7 9.5 %collective-permute-start.14 = (bf16[16,3072]{1,0:T(8,128)(2,1)S(1)}, bf16[16,3072]{1,0:T(8,128)(2,1)S(1)}, u32[]{:S(2)}, u32[]{:S(2)}) collective-permute-start(bf16[16,3072]{1,0:T(8,128)(2,1)S(1)} %get-tuple-element.76), channel_id=1, source_target_pairs={{0,8},{4,12},{8,0},{12,4},{1,9},{5,13},{9,1},{13,5},{2,10},{6,14},... | collective-permute-start | bytes 294920 | tf_op jit(solution)/shard_map/ppermute | solution.py:194
  36.6 8.6 %collective-permute-start.15 = (bf16[16,3072]{1,0:T(8,128)(2,1)S(1)}, bf16[16,3072]{1,0:T(8,128)(2,1)S(1)}, u32[]{:S(2)}, u32[]{:S(2)}) collective-permute-start(bf16[16,3072]{1,0:T(8,128)(2,1)S(1)} %get-tuple-element.77), channel_id=1, source_target_pairs={{0,12},{4,0},{8,4},{12,8},{1,13},{5,1},{9,5},{13,9},{2,14},{6,2},{... | collective-permute-start | bytes 294920 | tf_op jit(solution)/shard_map/ppermute | solution.py:194
  42.6 5.9 %collective-permute-start.12 = (bf16[64,512]{1,0:T(8,128)(2,1)S(1)}, bf16[64,512]{1,0:T(8,128)(2,1)S(1)}, u32[]{:S(2)}, u32[]{:S(2)}) collective-permute-start(bf16[64,512]{1,0:T(8,128)(2,1)S(1)} %get-tuple-element.68), channel_id=1, source_target_pairs={{0,16},{16,0},{32,48},{48,32},{64,80},{80,64},{96,112},{112,96},{1... | collective-permute-start | bytes 196616 | tf_op jit(solution)/shard_map/ppermute | solution.py:194

commit v4 on v3

--- a/solution.py
+++ b/solution.py
@@ -127,7 +127,8 @@
 
 
 def away(by):
-    return lax.rem(lax.axis_index("section") // 2 + (by + DEPTH), DEPTH)
+    sign = 1 - 2 * lax.rem(lax.axis_index("key"), 2)
+    return lax.rem(lax.axis_index("section") // 2 + by * sign + DEPTH, DEPTH)
 
 
 def total_of(*terms):
@@ -181,21 +182,28 @@
         o[...] = all_ref[lax.rem(me + by, 4)]
 
 
-def finish_kernel(keep_ref, *refs):
-    got, parts, (key_ref, value_ref, input_ref) = refs[0], refs[1:5], refs[5:]
-    total = total_of(keep_ref[...], got[...])
+def input_kernel(*refs):
+    refs[4][...] = total_of(*(r[...] for r in refs[:4])).astype(BF16)
+
+
+def finish_kernel(keep_ref, got_ref, key_ref, value_ref):
     width = key_ref.shape[1]
-    key_ref[...] = total[:, :width]
-    value_ref[...] = total[:, width:]
-    input_ref[...] = total_of(*(r[...] for r in parts)).astype(BF16)
+    key_ref[...] = total_of(keep_ref[:, :width], got_ref[:, :width])
+    value_ref[...] = total_of(keep_ref[:, width:], got_ref[:, width:])
 
 
 def moved(x, axis, to):
     return lax.ppermute(x, axis, [(i, to(i)) for i in range(lax.axis_size(axis))])
 
 
-def deeper(by, across=0):
-    return lambda section: (section // 2 + by) % DEPTH * 2 + (section % 2 ^ across)
+def sent(x, by):
+    sections, keys = lax.axis_size("section"), lax.axis_size("key")
+    pairs = []
+    for i in range(sections):
+        for k in range(keys):
+            depth = (i // 2 + (by if k % 2 == 0 else -by)) % DEPTH
+            pairs.append((i * keys + k, (depth * 2 + i % 2) * keys + k))
+    return lax.ppermute(x, ("section", "key"), pairs)
 
 
 def call(kernel, outs, ins, scratch=(), limit=16, specs=None, cost=1 << 28):
@@ -238,10 +246,10 @@
          near, near, on((slab, width), BF16), on((slab, width), BF16)],
         (*stats, e, dp, q, d),
     )
-    above = moved(near_down, "section", deeper(-1))
-    below = moved(near_up, "section", deeper(1))
-    far_k = moved(far_k, "section", deeper(-2))
-    far_v = moved(far_v, "section", deeper(2))
+    above = sent(near_down, -1)
+    below = sent(near_up, 1)
+    far_k = sent(far_k, -2)
+    far_v = sent(far_v, 2)
     parts = call(
         query_grad_kernel,
         [on((rows, heads * HD), BF16)] * 4, (ds, kt),
@@ -249,30 +257,31 @@
     )
     kv, parts = lax.optimization_barrier((kv, parts))
     parts = [parts[0]] + [moved(parts[by], "key", lambda i: i ^ by) for by in (1, 2, 3)]
-    whole = on((slab, 2 * width), BF16)
-    down, up, mine = call(
-        collect_kernel, [whole, whole, on((slab, 2 * width), F32)], (kv, above, below, far_k, far_v)
-    )
-    mine, parts = lax.optimization_barrier((mine, parts))
-    down = moved(down, "section", deeper(-2))
-    up = moved(up, "section", deeper(2))
     parts = call(
         project_kernel,
         [on((rows // 4, d_model), BF16)] * 4, (*parts, w),
         scratch=[on((4, rows // 4, d_model), BF16)],
     )
+    kv, parts = lax.optimization_barrier((kv, parts))
+    whole = on((slab, 2 * width), BF16)
+    down, up, mine = call(
+        collect_kernel, [whole, whole, on((slab, 2 * width), F32)], (kv, above, below, far_k, far_v)
+    )
+    down = sent(down, -2)
+    up = sent(up, 2)
     parts = [parts[0]] + [moved(parts[by], "head", lambda i: (i + by) % 4) for by in (1, 2, 3)]
     keep, send = call(
         last_join_kernel,
         [on((slab // 2, 2 * width), F32), on((slab // 2, 2 * width), BF16)], (mine, down, up),
         scratch=[on((2, slab // 2, 2 * width), F32)],
     )
-    got = moved(send, "section", deeper(0, 1))
-    key_grad, value_grad, input_grad = call(
+    got = moved(send, "section", lambda i: i ^ 1)
+    (input_grad,) = call(input_kernel, [jax.ShapeDtypeStruct((rows // 4, d_model), BF16)], parts)
+    got, input_grad = lax.optimization_barrier((got, input_grad))
+    key_grad, value_grad = call(
         finish_kernel,
-        [jax.ShapeDtypeStruct((slab // 2, width), F32), jax.ShapeDtypeStruct((slab // 2, width), F32),
-         jax.ShapeDtypeStruct((rows // 4, d_model), BF16)],
-        (keep, got, *parts),
+        [jax.ShapeDtypeStruct((slab // 2, width), F32), jax.ShapeDtypeStruct((slab // 2, width), F32)],
+        (keep, got),
     )
     return input_grad[None], key_grad, value_grad
 

time: 49.3 us -> 46.9 us (0.951)
  waiting for transfers between devices: 16.2 us -> 13 us
  Pallas kernels: 9.22 us -> 9.87 us
    ppermute x16 -> x10, starting transfers between devices: 23.1 us -> 11.7 us  [moved(): lax.ppermute(x, axis, [(i, to(i)) for i in range(lax.axis_size(axis))])]
    ppermute x0 -> x6, starting transfers between devices: none -> 11.4 us  [sent(): return lax.ppermute(x, ('section', 'key'), pairs)]
    ppermute x16 -> x10, waiting for transfers between devices: 16.2 us -> 7.63 us  [moved(): lax.ppermute(x, axis, [(i, to(i)) for i in range(lax.axis_size(axis))])]
    ppermute x0 -> x6, waiting for transfers between devices: none -> 5.35 us  [sent(): return lax.ppermute(x, ('section', 'key'), pairs)]
    pallas_call x7 -> x8, Pallas kernels: 9.22 us -> 9.87 us  [call(): pl.pallas_call(kernel, in_specs=specs or [VMEM] * len(ins), out_specs=[VM...]
  transfers between devices with their start and end apart: 16 -> 16, of which waited for: 8 -> 7; matrix products, arithmetic and copies ran while one was open for 0% -> 0% of each run, Pallas kernels for 5% -> 6%
where the time goes in v4:
time: 46.9 us; the launch traced here: 46.6 us
  starting transfers between devices  23.1 us (49%)
  waiting for transfers between devices  13 us (28%)
  Pallas kernels  9.87 us (21%)
  between operations  0.7 us (1%)
    ppermute x10, starting transfers between devices, moved(): lax.ppermute(x, axis, [(i, to(i)) for i in range(lax.axis_size(axis))])  11.7 us
    ppermute x6, starting transfers between devices, sent(): return lax.ppermute(x, ('section', 'key'), pairs)  11.4 us
    pallas_call x8, Pallas kernels, call(): pl.pallas_call(kernel, in_specs=specs or [VMEM] * len(ins), out_specs=[VM...  9.87 us
    ppermute x10, waiting for transfers between devices, moved(): lax.ppermute(x, axis, [(i, to(i)) for i in range(lax.axis_size(axis))])  7.63 us
    ppermute x6, waiting for transfers between devices, sent(): return lax.ppermute(x, ('section', 'key'), pairs)  5.35 us
  transfers between devices with their start and end apart: 16, of which 7 were waited for; matrix products, arithmetic and copies ran while one was open for 0% of the time, Pallas kernels for 6%

profile of v4, /device:TPU:8, one launch (start us, length us, event | category | flops | bytes accessed | tf_op | source)
XLA Modules:
  0.0 46.6 jit_solution(7290468349391664689)
XLA Ops:
  0.6 4.2 %shard_map.94 = (f32[6,1024,256]{2,1,0:T(8,128)S(1)}, f32[6,1024,256]{2,1,0:T(8,128)S(1)}, bf16[256,1024]{1,0:T(8,128)(2,1)S(1)}, f32[24,256]{1,0:T(8,128)S(1)},...) custom-call(s32[2,16]{1,0:T(2,128)} %bitcast.9, s32[2,16]{1,0:T(2,128)} %bitcast.10, ...), custom_call_target="tpu_custom_call" | custom-call | flops 268435456 | bytes 1048576 | tf_op jit(solution)/shard_map/pallas_call | solution.py:210
  4.8 1.0 %collective-permute-start.2 = (f32[24,256]{1,0:T(8,128)S(1)}, f32[24,256]{1,0:T(8,128)S(1)}, u32[]{:S(2)}, u32[]{:S(2)}) collective-permute-start(f32[24,256]{1,0:T(8,128)S(1)} %get-tuple-element.43.refs_0_), channel_id=1, source_target_pairs={{0,3},{1,2},{2,1},{3,0},{4,7},{5,6},{6,5},{7,4},{8,11},{9,10},{10,... | collective-permute-start | bytes 73736 | tf_op jit(solution)/shard_map/ppermute | solution.py:196
  6.8 1.6 %collective-permute-done.2.refs_3_ = f32[24,256]{1,0:T(8,128)S(1)} collective-permute-done((f32[24,256]{1,0:T(8,128)S(1)}, f32[24,256]{1,0:T(8,128)S(1)}, u32[]{:S(2)}, u32[]{:S(2)}) %collective-permute-start.2) | collective-permute-done | bytes 24608 | tf_op jit(solution)/shard_map/ppermute | solution.py:196
  8.4 1.3 %collective-permute-done.1.refs_2_ = f32[24,256]{1,0:T(8,128)S(1)} collective-permute-done((f32[24,256]{1,0:T(8,128)S(1)}, f32[24,256]{1,0:T(8,128)S(1)}, u32[]{:S(2)}, u32[]{:S(2)}) %collective-permute-start.1) | collective-permute-done | bytes 24608 | tf_op jit(solution)/shard_map/ppermute | solution.py:196
  9.7 1.9 %shard_map.95 = (bf16[6,1024,256]{2,1,0:T(8,128)(2,1)S(1)}, bf16[8,128,512]{2,1,0:T(8,128)(2,1)S(1)}, bf16[2,128,512]{2,1,0:T(8,128)(2,1)S(1)}, bf16[2,128,512]{...) custom-call(f32[24,256]{1,0:T(8,128)S(1)} %get-tuple-element.43.refs_0_, ...), custom_call_target="tpu_custom_call" | custom-call | flops 268435456 | bytes 1048576 | tf_op jit(solution)/shard_map/pallas_call | solution.py:210
  11.6 5.9 %collective-permute-start.6 = (bf16[2,128,512]{2,1,0:T(8,128)(2,1)S(1)}, bf16[2,128,512]{2,1,0:T(8,128)(2,1)S(1)}, u32[]{:S(2)}, u32[]{:S(2)}) collective-permute-start(bf16[2,128,512]{2,1,0:T(8,128)(2,1)S(1)} %get-tuple-element.66), channel_id=1, source_target_pairs={{0,224},{1,33},{2,226},{3,35},{16,240},{17,49},{18,242},{19,51},{3... | collective-permute-start | bytes 786440 | tf_op jit(solution)/shard_map/ppermute | solution.py:206
  17.5 0.7 %shard_map.96 = (bf16[64,768]{1,0:T(8,128)(2,1)S(1)}, bf16[64,768]{1,0:T(8,128)(2,1)S(1)}, bf16[64,768]{1,0:T(8,128)(2,1)S(1)}, bf16[64,768]{1,0:T(8,128)(2,1)S(1)}) custom-call(bf16[6,1024,256]{2,1,0:T(8,128)(2,1)S(1)} %get-tuple-element.49.ds_ref, bf16[256,1024]{1,0:T(8,128)(2,1)S(1)} %get-tuple-element.50.kt_ref), custom_call_target="tpu_custom_call" | custom-call | flops 268435456 | bytes 1048576 | tf_op jit(solution)/shard_map/pallas_call | solution.py:210
  18.3 0.9 %collective-permute-start.4 = (bf16[64,768]{1,0:T(8,128)(2,1)S(1)}, bf16[64,768]{1,0:T(8,128)(2,1)S(1)}, u32[]{:S(2)}, u32[]{:S(2)}) collective-permute-start(bf16[64,768]{1,0:T(8,128)(2,1)S(1)} %get-tuple-element.58), channel_id=1, source_target_pairs={{0,2},{1,3},{2,0},{3,1},{4,6},{5,7},{6,4},{7,5},{8,10},{9,11},{10,... | collective-permute-start | bytes 294920 | tf_op jit(solution)/shard_map/ppermute | solution.py:196
  19.2 1.0 %collective-permute-start.5 = (bf16[64,768]{1,0:T(8,128)(2,1)S(1)}, bf16[64,768]{1,0:T(8,128)(2,1)S(1)}, u32[]{:S(2)}, u32[]{:S(2)}) collective-permute-start(bf16[64,768]{1,0:T(8,128)(2,1)S(1)} %get-tuple-element.59), channel_id=1, source_target_pairs={{0,3},{1,2},{2,1},{3,0},{4,7},{5,6},{6,5},{7,4},{8,11},{9,10},{10,... | collective-permute-start | bytes 294920 | tf_op jit(solution)/shard_map/ppermute | solution.py:196
  20.2 2.5 %collective-permute-start.8 = (bf16[128,256]{1,0:T(8,128)(2,1)S(1)}, bf16[128,256]{1,0:T(8,128)(2,1)S(1)}, u32[]{:S(2)}, u32[]{:S(2)}) collective-permute-start(bf16[128,256]{1,0:T(8,128)(2,1)S(1)} %get-tuple-element.68), channel_id=1, source_target_pairs={{0,192},{1,65},{2,194},{3,67},{16,208},{17,81},{18,210},{19,83},{3... | collective-permute-start | bytes 196616 | tf_op jit(solution)/shard_map/ppermute | solution.py:206
  22.6 1.4 %collective-permute-done.4.c_ref = bf16[64,768]{1,0:T(8,128)(2,1)S(1)} collective-permute-done((bf16[64,768]{1,0:T(8,128)(2,1)S(1)}, bf16[64,768]{1,0:T(8,128)(2,1)S(1)}, u32[]{:S(2)}, u32[]{:S(2)}) %collective-permute-start.4) | collective-permute-done | bytes 98336 | tf_op jit(solution)/shard_map/ppermute | solution.py:196
  24.1 1.0 %collective-permute-done.5.d_ref = bf16[64,768]{1,0:T(8,128)(2,1)S(1)} collective-permute-done((bf16[64,768]{1,0:T(8,128)(2,1)S(1)}, bf16[64,768]{1,0:T(8,128)(2,1)S(1)}, u32[]{:S(2)}, u32[]{:S(2)}) %collective-permute-start.5) | collective-permute-done | bytes 98336 | tf_op jit(solution)/shard_map/ppermute | solution.py:196
  25.0 1.5 %shard_map.97 = (bf16[16,3072]{1,0:T(8,128)(2,1)S(1)}, bf16[16,3072]{1,0:T(8,128)(2,1)S(1)}, bf16[16,3072]{1,0:T(8,128)(2,1)S(1)}, bf16[16,3072]{1,0:T(8,128)(2,1)S(1)}) custom-call(bf16[64,768]{1,0:T(8,128)(2,1)S(1)} %get-tuple-element.56.a_ref, bf16[64,768]{1,0:T(8,128)(2,1)S(1)} %collective-permute-done.3.b_ref, ...), custom_call_target="tpu_custom_call" | custom-call | flops 268435456 | bytes 1048576 | tf_op jit(solution)/shard_map/pallas_call | solution.py:210
  26.6 3.9 %collective-permute-done.9.far_v = bf16[128,256]{1,0:T(8,128)(2,1)S(1)} collective-permute-done((bf16[128,256]{1,0:T(8,128)(2,1)S(1)}, bf16[128,256]{1,0:T(8,128)(2,1)S(1)}, u32[]{:S(2)}, u32[]{:S(2)}) %collective-permute-start.9) | collective-permute-done | bytes 65568 | tf_op jit(solution)/shard_map/ppermute | solution.py:206
  30.6 1.3 %collective-permute-start.10 = (bf16[128,512]{1,0:T(8,128)(2,1)S(1)}, bf16[128,512]{1,0:T(8,128)(2,1)S(1)}, u32[]{:S(2)}, u32[]{:S(2)}) collective-permute-start(bf16[128,512]{1,0:T(8,128)(2,1)S(1)} %get-tuple-element.71), channel_id=1, source_target_pairs={{0,192},{1,65},{2,194},{3,67},{16,208},{17,81},{18,210},{19,83},{3... | collective-permute-start | bytes 393224 | tf_op jit(solution)/shard_map/ppermute | solution.py:206
  31.9 1.7 %collective-permute-start.11 = (bf16[128,512]{1,0:T(8,128)(2,1)S(1)}, bf16[128,512]{1,0:T(8,128)(2,1)S(1)}, u32[]{:S(2)}, u32[]{:S(2)}) collective-permute-start(bf16[128,512]{1,0:T(8,128)(2,1)S(1)} %get-tuple-element.72), channel_id=1, source_target_pairs={{0,64},{1,193},{2,66},{3,195},{16,80},{17,209},{18,82},{19,211},{3... | collective-permute-start | bytes 393224 | tf_op jit(solution)/shard_map/ppermute | solution.py:206
  33.6 1.6 %collective-permute-start.13 = (bf16[16,3072]{1,0:T(8,128)(2,1)S(1)}, bf16[16,3072]{1,0:T(8,128)(2,1)S(1)}, u32[]{:S(2)}, u32[]{:S(2)}) collective-permute-start(bf16[16,3072]{1,0:T(8,128)(2,1)S(1)} %get-tuple-element.75), channel_id=1, source_target_pairs={{0,4},{4,8},{8,12},{12,0},{1,5},{5,9},{9,13},{13,1},{2,6},{6,10},{... | collective-permute-start | bytes 294920 | tf_op jit(solution)/shard_map/ppermute | solution.py:196
  35.2 0.9 %collective-permute-start.14 = (bf16[16,3072]{1,0:T(8,128)(2,1)S(1)}, bf16[16,3072]{1,0:T(8,128)(2,1)S(1)}, u32[]{:S(2)}, u32[]{:S(2)}) collective-permute-start(bf16[16,3072]{1,0:T(8,128)(2,1)S(1)} %get-tuple-element.76), channel_id=1, source_target_pairs={{0,8},{4,12},{8,0},{12,4},{1,9},{5,13},{9,1},{13,5},{2,10},{6,14},... | collective-permute-start | bytes 294920 | tf_op jit(solution)/shard_map/ppermute | solution.py:196
  36.2 2.4 %collective-permute-start.15 = (bf16[16,3072]{1,0:T(8,128)(2,1)S(1)}, bf16[16,3072]{1,0:T(8,128)(2,1)S(1)}, u32[]{:S(2)}, u32[]{:S(2)}) collective-permute-start(bf16[16,3072]{1,0:T(8,128)(2,1)S(1)} %get-tuple-element.77), channel_id=1, source_target_pairs={{0,12},{4,0},{8,4},{12,8},{1,13},{5,1},{9,5},{13,9},{2,14},{6,2},{... | collective-permute-start | bytes 294920 | tf_op jit(solution)/shard_map/ppermute | solution.py:196
  38.6 1.5 %collective-permute-done.11.up_ref = bf16[128,512]{1,0:T(8,128)(2,1)S(1)} collective-permute-done((bf16[128,512]{1,0:T(8,128)(2,1)S(1)}, bf16[128,512]{1,0:T(8,128)(2,1)S(1)}, u32[]{:S(2)}, u32[]{:S(2)}) %collective-permute-start.11) | collective-permute-done | bytes 131104 | tf_op jit(solution)/shard_map/ppermute | solution.py:206
  40.1 2.8 %collective-permute-start.12 = (bf16[64,512]{1,0:T(8,128)(2,1)S(1)}, bf16[64,512]{1,0:T(8,128)(2,1)S(1)}, u32[]{:S(2)}, u32[]{:S(2)}) collective-permute-start(bf16[64,512]{1,0:T(8,128)(2,1)S(1)} %get-tuple-element.73), channel_id=1, source_target_pairs={{0,16},{16,0},{32,48},{48,32},{64,80},{80,64},{96,112},{112,96},{1... | collective-permute-start | bytes 196616 | tf_op jit(solution)/shard_map/ppermute | solution.py:196
  42.9 0.7 %shard_map.100 = bf16[16,3072]{1,0:T(8,128)(2,1)} custom-call(bf16[16,3072]{1,0:T(8,128)(2,1)S(1)} %get-tuple-element.74.refs_0_, bf16[16,3072]{1,0:T(8,128)(2,1)S(1)} %collective-permute-done.13.refs_1_, bf16[16,3072]{1,0:T(8,128)(2,1)S(1)} %collective-permute-done.14.refs_2_, bf16[16,3072]{1,0:T(8,128)(2,1)S(1)} %collective-permute-done.15.refs_3_), custom_call_target="tpu_custom_call" | custom-call | flops 268435456 | bytes 1048576 | tf_op jit(solution)/shard_map/pallas_call | solution.py:210
  43.6 2.3 %collective-permute-done.12.got_ref = bf16[64,512]{1,0:T(8,128)(2,1)S(1)} collective-permute-done((bf16[64,512]{1,0:T(8,128)(2,1)S(1)}, bf16[64,512]{1,0:T(8,128)(2,1)S(1)}, u32[]{:S(2)}, u32[]{:S(2)}) %collective-permute-start.12) | collective-permute-done | bytes 65568 | tf_op jit(solution)/shard_map/ppermute | solution.py:196
  45.9 0.7 %shard_map.101 = (f32[64,256]{1,0:T(8,128)}, f32[64,256]{1,0:T(8,128)}) custom-call(f32[64,512]{1,0:T(8,128)S(1)} %get-tuple-element.79.keep_ref, bf16[64,512]{1,0:T(8,128)(2,1)S(1)} %collective-permute-done.12.got_ref), custom_call_target="tpu_custom_call" | custom-call | flops 268435456 | bytes 1048576 | tf_op jit(solution)/shard_map/pallas_call | solution.py:210
  (16 shorter events, 1.3 us)
Async XLA Ops:
  4.8 3.6 %collective-permute-start.2 = (f32[24,256]{1,0:T(8,128)S(1)}, f32[24,256]{1,0:T(8,128)S(1)}, u32[]{:S(2)}, u32[]{:S(2)}) collective-permute-start(f32[24,256]{1,0:T(8,128)S(1)} %get-tuple-element.43.refs_0_), channel_id=1, source_target_pairs={{0,3},{1,2},{2,1},{3,0},{4,7},{5,6},{6,5},{7,4},{8,11},{9,10},{10,... | collective-permute-start | bytes 73736 | tf_op jit(solution)/shard_map/ppermute | solution.py:196
  5.8 3.8 %collective-permute-start.1 = (f32[24,256]{1,0:T(8,128)S(1)}, f32[24,256]{1,0:T(8,128)S(1)}, u32[]{:S(2)}, u32[]{:S(2)}) collective-permute-start(f32[24,256]{1,0:T(8,128)S(1)} %get-tuple-element.43.refs_0_), channel_id=1, source_target_pairs={{0,2},{1,3},{2,0},{3,1},{4,6},{5,7},{6,4},{7,5},{8,10},{9,11},{10,... | collective-permute-start | bytes 73736 | tf_op jit(solution)/shard_map/ppermute | solution.py:196
  6.5 3.2 %collective-permute-start = (f32[24,256]{1,0:T(8,128)S(1)}, f32[24,256]{1,0:T(8,128)S(1)}, u32[]{:S(2)}, u32[]{:S(2)}) collective-permute-start(f32[24,256]{1,0:T(8,128)S(1)} %get-tuple-element.43.refs_0_), channel_id=1, source_target_pairs={{0,1},{1,0},{2,3},{3,2},{4,5},{5,4},{6,7},{7,6},{8,9},{9,8},{10,11... | collective-permute-start | bytes 73736 | tf_op jit(solution)/shard_map/ppermute | solution.py:196
  11.6 18.9 %collective-permute-start.6 = (bf16[2,128,512]{2,1,0:T(8,128)(2,1)S(1)}, bf16[2,128,512]{2,1,0:T(8,128)(2,1)S(1)}, u32[]{:S(2)}, u32[]{:S(2)}) collective-permute-start(bf16[2,128,512]{2,1,0:T(8,128)(2,1)S(1)} %get-tuple-element.66), channel_id=1, source_target_pairs={{0,224},{1,33},{2,226},{3,35},{16,240},{17,49},{18,242},{19,51},{3... | collective-permute-start | bytes 786440 | tf_op jit(solution)/shard_map/ppermute | solution.py:206
  17.5 13.0 %collective-permute-start.7 = (bf16[2,128,512]{2,1,0:T(8,128)(2,1)S(1)}, bf16[2,128,512]{2,1,0:T(8,128)(2,1)S(1)}, u32[]{:S(2)}, u32[]{:S(2)}) collective-permute-start(bf16[2,128,512]{2,1,0:T(8,128)(2,1)S(1)} %get-tuple-element.67), channel_id=1, source_target_pairs={{0,32},{1,225},{2,34},{3,227},{16,48},{17,241},{18,50},{19,243},{3... | collective-permute-start | bytes 786440 | tf_op jit(solution)/shard_map/ppermute | solution.py:206
  18.2 2.0 %collective-permute-start.3 = (bf16[64,768]{1,0:T(8,128)(2,1)S(1)}, bf16[64,768]{1,0:T(8,128)(2,1)S(1)}, u32[]{:S(2)}, u32[]{:S(2)}) collective-permute-start(bf16[64,768]{1,0:T(8,128)(2,1)S(1)} %get-tuple-element.57), channel_id=1, source_target_pairs={{0,1},{1,0},{2,3},{3,2},{4,5},{5,4},{6,7},{7,6},{8,9},{9,8},{10,11... | collective-permute-start | bytes 294920 | tf_op jit(solution)/shard_map/ppermute | solution.py:196
  18.3 5.8 %collective-permute-start.4 = (bf16[64,768]{1,0:T(8,128)(2,1)S(1)}, bf16[64,768]{1,0:T(8,128)(2,1)S(1)}, u32[]{:S(2)}, u32[]{:S(2)}) collective-permute-start(bf16[64,768]{1,0:T(8,128)(2,1)S(1)} %get-tuple-element.58), channel_id=1, source_target_pairs={{0,2},{1,3},{2,0},{3,1},{4,6},{5,7},{6,4},{7,5},{8,10},{9,11},{10,... | collective-permute-start | bytes 294920 | tf_op jit(solution)/shard_map/ppermute | solution.py:196
  19.2 5.9 %collective-permute-start.5 = (bf16[64,768]{1,0:T(8,128)(2,1)S(1)}, bf16[64,768]{1,0:T(8,128)(2,1)S(1)}, u32[]{:S(2)}, u32[]{:S(2)}) collective-permute-start(bf16[64,768]{1,0:T(8,128)(2,1)S(1)} %get-tuple-element.59), channel_id=1, source_target_pairs={{0,3},{1,2},{2,1},{3,0},{4,7},{5,6},{6,5},{7,4},{8,11},{9,10},{10,... | collective-permute-start | bytes 294920 | tf_op jit(solution)/shard_map/ppermute | solution.py:196
  20.2 6.4 %collective-permute-start.8 = (bf16[128,256]{1,0:T(8,128)(2,1)S(1)}, bf16[128,256]{1,0:T(8,128)(2,1)S(1)}, u32[]{:S(2)}, u32[]{:S(2)}) collective-permute-start(bf16[128,256]{1,0:T(8,128)(2,1)S(1)} %get-tuple-element.68), channel_id=1, source_target_pairs={{0,192},{1,65},{2,194},{3,67},{16,208},{17,81},{18,210},{19,83},{3... | collective-permute-start | bytes 196616 | tf_op jit(solution)/shard_map/ppermute | solution.py:206
  24.1 6.4 %collective-permute-start.9 = (bf16[128,256]{1,0:T(8,128)(2,1)S(1)}, bf16[128,256]{1,0:T(8,128)(2,1)S(1)}, u32[]{:S(2)}, u32[]{:S(2)}) collective-permute-start(bf16[128,256]{1,0:T(8,128)(2,1)S(1)} %get-tuple-element.69), channel_id=1, source_target_pairs={{0,64},{1,193},{2,66},{3,195},{16,80},{17,209},{18,82},{19,211},{3... | collective-permute-start | bytes 196616 | tf_op jit(solution)/shard_map/ppermute | solution.py:206
  30.6 7.9 %collective-permute-start.10 = (bf16[128,512]{1,0:T(8,128)(2,1)S(1)}, bf16[128,512]{1,0:T(8,128)(2,1)S(1)}, u32[]{:S(2)}, u32[]{:S(2)}) collective-permute-start(bf16[128,512]{1,0:T(8,128)(2,1)S(1)} %get-tuple-element.71), channel_id=1, source_target_pairs={{0,192},{1,65},{2,194},{3,67},{16,208},{17,81},{18,210},{19,83},{3... | collective-permute-start | bytes 393224 | tf_op jit(solution)/shard_map/ppermute | solution.py:206
  31.9 8.1 %collective-permute-start.11 = (bf16[128,512]{1,0:T(8,128)(2,1)S(1)}, bf16[128,512]{1,0:T(8,128)(2,1)S(1)}, u32[]{:S(2)}, u32[]{:S(2)}) collective-permute-start(bf16[128,512]{1,0:T(8,128)(2,1)S(1)} %get-tuple-element.72), channel_id=1, source_target_pairs={{0,64},{1,193},{2,66},{3,195},{16,80},{17,209},{18,82},{19,211},{3... | collective-permute-start | bytes 393224 | tf_op jit(solution)/shard_map/ppermute | solution.py:206
  33.6 9.3 %collective-permute-start.13 = (bf16[16,3072]{1,0:T(8,128)(2,1)S(1)}, bf16[16,3072]{1,0:T(8,128)(2,1)S(1)}, u32[]{:S(2)}, u32[]{:S(2)}) collective-permute-start(bf16[16,3072]{1,0:T(8,128)(2,1)S(1)} %get-tuple-element.75), channel_id=1, source_target_pairs={{0,4},{4,8},{8,12},{12,0},{1,5},{5,9},{9,13},{13,1},{2,6},{6,10},{... | collective-permute-start | bytes 294920 | tf_op jit(solution)/shard_map/ppermute | solution.py:196
  35.2 7.7 %collective-permute-start.14 = (bf16[16,3072]{1,0:T(8,128)(2,1)S(1)}, bf16[16,3072]{1,0:T(8,128)(2,1)S(1)}, u32[]{:S(2)}, u32[]{:S(2)}) collective-permute-start(bf16[16,3072]{1,0:T(8,128)(2,1)S(1)} %get-tuple-element.76), channel_id=1, source_target_pairs={{0,8},{4,12},{8,0},{12,4},{1,9},{5,13},{9,1},{13,5},{2,10},{6,14},... | collective-permute-start | bytes 294920 | tf_op jit(solution)/shard_map/ppermute | solution.py:196
  36.2 6.8 %collective-permute-start.15 = (bf16[16,3072]{1,0:T(8,128)(2,1)S(1)}, bf16[16,3072]{1,0:T(8,128)(2,1)S(1)}, u32[]{:S(2)}, u32[]{:S(2)}) collective-permute-start(bf16[16,3072]{1,0:T(8,128)(2,1)S(1)} %get-tuple-element.77), channel_id=1, source_target_pairs={{0,12},{4,0},{8,4},{12,8},{1,13},{5,1},{9,5},{13,9},{2,14},{6,2},{... | collective-permute-start | bytes 294920 | tf_op jit(solution)/shard_map/ppermute | solution.py:196
  40.1 5.9 %collective-permute-start.12 = (bf16[64,512]{1,0:T(8,128)(2,1)S(1)}, bf16[64,512]{1,0:T(8,128)(2,1)S(1)}, u32[]{:S(2)}, u32[]{:S(2)}) collective-permute-start(bf16[64,512]{1,0:T(8,128)(2,1)S(1)} %get-tuple-element.73), channel_id=1, source_target_pairs={{0,16},{16,0},{32,48},{48,32},{64,80},{80,64},{96,112},{112,96},{1... | collective-permute-start | bytes 196616 | tf_op jit(solution)/shard_map/ppermute | solution.py:196
